TPU v7x, 256 devices: a whole 4x4x8 slice. The times are simulated.
256 devices in a mesh: tile: 32 (over x, z), ens: 8 (over y, core).
Axes of the slice: x: 4, y: 4, z: 8, core: 2. Of those that a mesh axis runs over, the one named last changes fastest.
Arguments:
- initial_sample_set: float32 [80, 2, 128, 2048], P('ens', None, 'tile'), may hold values from -6 to 6
- flow_velocity: float32 [2, 2, 128, 2048], P(None, None, 'tile'), may hold values from -0.4 to 0.4
- obs_loc: int32 [3, 2, 32768], P(None, None, 'tile'), may hold values from 0 to 2047, as said below
- obs_count: int32 [2, 32], P(None, 'tile'), may hold values from 256 to 1024, as said below
- obs_value: float32 [2, 32768], P(None, 'tile'), may hold values from -6 to 6
- obs_error: float32 [2, 32768], P(None, 'tile'), may hold values from 0.25 to 2
Outputs:
- analysis: float32 [80, 2, 128, 2048], P('ens', None, 'tile')
Inputs may be any that keep to these rules, and one draw needn't show every extreme that they name: `obs_loc`: slots 1024 * t to 1024 * (t + 1) - 1 of a batch belong to tile t: their row lies in rows 4 * t to 4 * (t + 1) - 1; columns lie in 0 to 2047 and levels in 0 to 1. `obs_count`: in every batch some tile has exactly 1024 live observations; a tile's live observations are its first slots.
All inputs are finite; a program needn't handle non-finite values.
Results may differ from a plain program's by a relative error of at most 0.0003.
Values sent between devices are 32-bit elements; how exact they have to be, the bound alone decides.
A program may use at most 128 MiB of HBM per device.

v0:
```python
import jax
import jax.numpy as jnp
from jax import lax
from jax.sharding import PartitionSpec as P

BATCHES = 2
REACH = 2


SPREAD_RATE = 0.05
EPSILON = 1e-06
PRECISE = lax.Precision.HIGHEST


def with_halo(cells, sides, width):
    for axis, dim in sides:
        count = lax.axis_size(axis)
        ends = count - 1
        head = lax.slice_in_dim(cells, 0, width, axis=dim)
        tail = lax.slice_in_dim(cells, cells.shape[dim] - width, cells.shape[dim], axis=dim)
        cells = jnp.concatenate(
            [
                lax.ppermute(tail, axis, [(i, (i + 1) % count) for i in range(ends)]),
                cells,
                lax.ppermute(head, axis, [((i + 1) % count, i) for i in range(ends)]),
            ],
            axis=dim,
        )
    return cells


def shifted(value, axis, steps):
    count = lax.axis_size(axis)
    leading, last = (max(0, -steps), min(count, count - steps))
    return lax.ppermute(value, axis, [(source, source + steps) for source in range(leading, last)])


def advance(centre, row_above, row_below, col_left, col_right, flow_velocity):
    wind_rows = flow_velocity[0][None]
    wind_cols = flow_velocity[1][None]
    tendency = (
        jnp.maximum(wind_rows, 0.0) * (centre - row_above)
        + jnp.minimum(wind_rows, 0.0) * (row_below - centre)
        + jnp.maximum(wind_cols, 0.0) * (centre - col_left)
        + jnp.minimum(wind_cols, 0.0) * (col_right - centre)
    )
    return (
        centre
        - tendency
        + SPREAD_RATE * (row_above + row_below + col_left + col_right - 4.0 * centre)
    )


def increments(prior_obs, row_values, error_row, live_mask):
    members = prior_obs.shape[0]
    average = jnp.sum(prior_obs, axis=0) / members
    deviation = prior_obs - average[None, :]
    var_prior = jnp.sum(deviation * deviation, axis=0) / (members - 1) + EPSILON
    combined = var_prior + error_row
    shrink_factor = jnp.sqrt(error_row / combined)
    mean_post = (error_row * average + var_prior * row_values) / combined
    obs_shift = live_mask[None, :] * (
        (shrink_factor - 1.0)[None, :] * deviation + (mean_post - average)[None, :]
    )
    weight = live_mask[None, :] * deviation / ((members - 1) * var_prior)[None, :]
    return (weight, obs_shift)


def block_gain(
    states, weight, obs_shift, obs_place, cell_lev, cell_row, cell_col, radius, col_radius
):
    covariance = lax.dot_general(
        weight,
        states,
        (((0,), (0,)), ((), ())),
        precision=PRECISE,
        preferred_element_type=jnp.float32,
    )
    row_gap = cell_row[None, :] - obs_place[0][:, None]
    column_spacing = cell_col[None, :] - obs_place[1][:, None]
    level_gap = jnp.abs(cell_lev[None, :] - obs_place[2][:, None])
    closeness = jnp.maximum(
        1.0
        - row_gap * row_gap / (radius * radius)
        - column_spacing * column_spacing / (col_radius * col_radius),
        0.0,
    )
    gain_map = covariance * (closeness * closeness / (1.0 + level_gap))
    return jnp.dot(obs_shift, gain_map, precision=PRECISE, preferred_element_type=jnp.float32)


def propagate_model(initial_sample_set, flow_velocity):
    padded = with_halo(initial_sample_set, (("tile", 2),), 1)
    padded = jnp.pad(padded, ((0, 0), (0, 0), (0, 0), (1, 1)))
    return advance(
        padded[:, :, 1:-1, 1:-1],
        padded[:, :, :-2, 1:-1],
        padded[:, :, 2:, 1:-1],
        padded[:, :, 1:-1, :-2],
        padded[:, :, 1:-1, 2:],
        flow_velocity,
    )


def analyse(
    columns,
    prior_obs,
    obs_place,
    row_values,
    error_row,
    live_mask,
    cell_lev,
    cell_row,
    cell_col,
    radius,
    col_radius,
):
    weight, obs_shift = increments(prior_obs, row_values, error_row, live_mask)
    payload = (weight, obs_shift, obs_place)
    received = [payload]
    for displacement in range(1, REACH + 1):
        received.append(shifted((payload[0], payload[1], payload[2]), "tile", displacement))
        received.append(shifted((payload[0], payload[1], payload[2]), "tile", -displacement))
    members = columns.shape[0]
    flat_state = columns.reshape(members, -1)
    increment = jnp.zeros_like(flat_state)
    for incoming in received:
        increment = increment + block_gain(
            flat_state,
            incoming[0],
            incoming[1],
            incoming[2],
            cell_lev,
            cell_row,
            cell_col,
            radius,
            col_radius,
        )
    return columns + increment.reshape(columns.shape)


def on_device(initial_sample_set, flow_velocity, obs_loc, obs_count, obs_value, obs_error):
    member_deviation, levels, row_count, col_total = initial_sample_set.shape
    ens_size = lax.axis_size("ens")
    col_count = col_total // ens_size
    obs_tile = obs_value.shape[1]
    tile_index = lax.axis_index("tile")
    ens_index = lax.axis_index("ens")
    radius = float(REACH * row_count)
    col_radius = float(col_total // 2)
    current_model_vector = propagate_model(initial_sample_set, flow_velocity)
    slots = jnp.arange(obs_tile, dtype=jnp.int32)
    cell_index = jnp.arange(levels * row_count * col_count, dtype=jnp.int32)
    cell_lev = (cell_index // (row_count * col_count)).astype(jnp.float32)
    cell_row = (tile_index * row_count + cell_index // col_count % row_count).astype(jnp.float32)
    cell_col = (ens_index * col_count + cell_index % col_count).astype(jnp.float32)
    for batch_index in range(BATCHES):
        local_row = obs_loc[0, batch_index] - tile_index * row_count
        flat_index = (obs_loc[2, batch_index] * row_count + local_row) * col_total + obs_loc[
            1, batch_index
        ]
        own_prior = jnp.take(current_model_vector.reshape(member_deviation, -1), flat_index, axis=1)
        prior_obs = lax.all_gather(own_prior, "ens", axis=0, tiled=True)
        columns = lax.all_to_all(
            current_model_vector, "ens", split_axis=3, concat_axis=0, tiled=True
        )
        live_mask = (slots < obs_count[batch_index, 0]).astype(jnp.float32)
        obs_place = obs_loc[:, batch_index].astype(jnp.float32)
        columns = analyse(
            columns,
            prior_obs,
            obs_place,
            obs_value[batch_index],
            obs_error[batch_index],
            live_mask,
            cell_lev,
            cell_row,
            cell_col,
            radius,
            col_radius,
        )
        current_model_vector = lax.all_to_all(
            columns, "ens", split_axis=0, concat_axis=3, tiled=True
        )
    return current_model_vector


def solution(mesh):
    in_specs = (
        P("ens", None, "tile", None),
        P(None, None, "tile", None),
        P(None, None, "tile"),
        P(None, "tile"),
        P(None, "tile"),
        P(None, "tile"),
    )
    out_specs = P("ens", None, "tile", None)
    return jax.shard_map(
        on_device, mesh=mesh, in_specs=in_specs, out_specs=out_specs, check_vma=False
    )
```

profile of v0, /device:TPU:2, one launch (start us, length us, event | category | flops | bytes accessed | tf_op | source)
XLA Modules:
  0.0 487.8 jit_solution(17337714978346496619)
XLA Ops:
  0.9 8.2 %collective-permute-start.13 = (f32[3,1024]{1,0:T(4,128)S(1)}, f32[3,1024]{1,0:T(4,128)S(1)}, u32[]{:S(2)}, u32[]{:S(2)}) collective-permute-start(f32[3,1024]{1,0:T(4,128)S(1)} %bitcast.143), channel_id=1, source_target_pairs={{16,0},{24,8},{32,16},{40,24},{48,32},{56,40},{64,48},{72,56},{80,... | collective-permute-start | bytes 36872 | tf_op jit(solution)/shard_map/ppermute | solution.py:35
  32.5 8.1 %collective-permute-start.19 = (f32[3,1024]{1,0:T(4,128)S(1)}, f32[3,1024]{1,0:T(4,128)S(1)}, u32[]{:S(2)}, u32[]{:S(2)}) collective-permute-start(f32[3,1024]{1,0:T(4,128)S(1)} %bitcast.141), channel_id=1, source_target_pairs={{8,0},{16,8},{24,16},{32,24},{40,32},{48,40},{56,48},{64,56},{72,6... | collective-permute-start | bytes 36872 | tf_op jit(solution)/shard_map/ppermute | solution.py:35
  82.1 13.6 %all-gather = f32[8,10,1024]{2,1,0:T(8,128)S(1)} all-gather(f32[1,10,1024]{2,1,0:T(8,128)S(1)} %copy.137), channel_id=1, replica_groups=mesh['tile'=32,'ens'=8] {'ens'}, dimensions={0}, use_global_device_ids=true | all-gather | bytes 368640 | tf_op jit(solution)/shard_map/all_gather | solution.py:163
  95.8 12.3 %reshape.233 = f32[8,1,20480]{2,1,0:T(1,128)} reshape(f32[2048,2,4,10]{3,2,1,0:T(4,128)} %bitcast.120) | data formatting | bytes 1310720
  116.1 7.4 %all-to-all-done = f32[8,1,20480]{2,1,0:T(1,128)S(1)} async-done(((f32[8,1,20480]{2,1,0:T(1,128)}), f32[8,1,20480]{2,1,0:T(1,128)S(1)}, u32[]{:S(2)}, u32[]{:S(2)}) %all-to-all-start) | async-done | bytes 655392 | tf_op jit(solution)/shard_map/all_to_all | solution.py:164
  126.3 14.6 %reshape.234 = f32[2048,2,4,10]{3,2,1,0:T(4,128)} reshape(f32[8,20480]{1,0:T(8,128)S(1)} %reduce.2) | data formatting | bytes 1310720
  155.4 9.7 %fusion.144 = f32[80,2048]{1,0:T(8,128)S(1)} fusion(f32[80,1024]{1,0:T(8,128)S(1)} %get-tuple-element.11, f32[1024,2048]{1,0:T(8,128)S(1)} %fusion.370, f32[1024]{0:T(1024)S(1)} %bitcast.153, f32[2048]{0:T(1024)S(1)} %get-tuple-element.64, f32[1024]{0:T(1024)S(1)} %bitcast.152, f32[2048]{0:T(1024)S(1)} %fusion.311, f32[1024]{0:T(1024)S(1)} %bitcast.154, ...), kind=kOutput, calls=%fused_computation.146 | convolution fusion | flops 2044723200 | bytes 9408512 | tf_op jit(solution)/shard_map/dot_general | solution.py:89
  176.2 9.6 %fusion.80 = f32[80,2048]{1,0:T(8,128)S(1)} fusion(f32[80,1024]{1,0:T(8,128)S(1)} %collective-permute-done.11, f32[1024,2048]{1,0:T(8,128)S(1)} %fusion.374, f32[1024]{0:T(1024)S(1)} %bitcast.171, f32[1024]{0:T(1024)S(1)} %bitcast.172, f32[1024]{0:T(1024)S(1)} %bitcast.170, f32[2048]{0:T(1024)S(1)} %get-tuple-element.64, f32[2048]{0:T(1024)S(1)} %fusion.311, ...), kind=kOutput, calls=%fused_computation.82 | convolution fusion | flops 2044723200 | bytes 9408512 | tf_op jit(solution)/shard_map/dot_general | solution.py:89
  185.8 13.4 %collective-permute-done.9 = f32[80,1024]{1,0:T(8,128)S(1)} collective-permute-done((f32[80,1024]{1,0:T(8,128)S(1)}, f32[80,1024]{1,0:T(8,128)S(1)}, u32[]{:S(2)}, u32[]{:S(2)}) %collective-permute-start.9) | collective-permute-done | bytes 327712 | tf_op jit(solution)/shard_map/ppermute | solution.py:35
  210.8 9.6 %fusion.96 = f32[80,2048]{1,0:T(8,128)S(1)} fusion(f32[80,1024]{1,0:T(8,128)S(1)} %collective-permute-done.8, f32[1024,2048]{1,0:T(8,128)S(1)} %fusion.373, f32[1024]{0:T(1024)S(1)} %bitcast.165, f32[1024]{0:T(1024)S(1)} %bitcast.166, f32[1024]{0:T(1024)S(1)} %bitcast.164, f32[2048]{0:T(1024)S(1)} %get-tuple-element.64, f32[2048]{0:T(1024)S(1)} %fusion.311, ...), kind=kOutput, calls=%fused_computation.98 | convolution fusion | flops 2044723200 | bytes 9408512 | tf_op jit(solution)/shard_map/dot_general | solution.py:89
  235.5 9.6 %fusion.112 = f32[80,2048]{1,0:T(8,128)S(1)} fusion(f32[80,1024]{1,0:T(8,128)S(1)} %collective-permute-done.5, f32[1024,2048]{1,0:T(8,128)S(1)} %fusion.372, f32[1024]{0:T(1024)S(1)} %bitcast.162, f32[1024]{0:T(1024)S(1)} %bitcast.163, f32[1024]{0:T(1024)S(1)} %bitcast.161, f32[2048]{0:T(1024)S(1)} %get-tuple-element.64, f32[2048]{0:T(1024)S(1)} %fusion.311, ...), kind=kOutput, calls=%fused_computation.114 | convolution fusion | flops 2044723200 | bytes 9408512 | tf_op jit(solution)/shard_map/dot_general | solution.py:89
  252.4 9.8 %fusion.269 = f32[80,2048]{1,0:T(8,128)S(1)} fusion(f32[80,2048]{1,0:T(8,128)S(1)} %fusion.80, f32[80,2048]{1,0:T(8,128)S(1)} %fusion.96, f32[80,2048]{1,0:T(8,128)S(1)} %fusion.112, f32[80,2048]{1,0:T(8,128)S(1)} %fusion.144, f32[80,1024]{1,0:T(8,128)S(1)} %collective-permute-done.2, f32[1024,2048]{1,0:T(8,128)S(1)} %fusion.371, f32[1024]{0:T(1024)S(1)} %bitcast.159, ...), kind=kOutput, calls=%fused_computation.265 | convolution fusion | flops 2045378560 | bytes 12029952 | tf_op jit(solution)/shard_map/dot_general | solution.py:89
  267.3 11.6 %all-to-all-done.1 = f32[80,2,4,256]{3,2,1,0:T(4,128)S(1)} async-done(((f32[80,2,4,256]{3,2,1,0:T(4,128)}), f32[80,2,4,256]{3,2,1,0:T(4,128)S(1)}, u32[]{:S(2)}, u32[]{:S(2)}) %all-to-all-start.1) | async-done | bytes 655392 | tf_op jit(solution)/shard_map/all_to_all | solution.py:182
  290.2 13.1 %all-gather.1 = f32[8,10,1024]{2,1,0:T(8,128)S(1)} all-gather(f32[1,10,1024]{2,1,0:T(8,128)S(1)} %copy.142), channel_id=1, replica_groups=mesh['tile'=32,'ens'=8] {'ens'}, dimensions={0}, use_global_device_ids=true | all-gather | bytes 368640 | tf_op jit(solution)/shard_map/all_gather | solution.py:163
  303.4 12.0 %copy.139 = f32[10,2,4,8,256]{0,2,1,4,3:T(4,128)} copy(f32[10,2,4,8,256]{0,4,3,2,1:T(8,128)} %bitcast.119) | data formatting | bytes 1310720 | tf_op jit(solution)/shard_map/all_to_all | solution.py:182
  315.4 12.2 %reshape.235 = f32[8,1,20480]{2,1,0:T(1,128)} reshape(f32[2048,2,4,10]{3,2,1,0:T(4,128)} %bitcast.122) | data formatting | bytes 1310720
  345.8 7.6 %collective-permute-start.17 = (f32[80,1024]{1,0:T(8,128)S(1)}, f32[80,1024]{1,0:T(8,128)S(1)}, u32[]{:S(2)}, u32[]{:S(2)}) collective-permute-start(f32[80,1024]{1,0:T(8,128)S(1)} %get-tuple-element.9), channel_id=1, source_target_pairs={{8,0},{16,8},{24,16},{32,24},{40,32},{48,40},{56,48},{64,56},{72,6... | collective-permute-start | bytes 983048 | tf_op jit(solution)/shard_map/ppermute | solution.py:35
  355.6 14.6 %reshape.236 = f32[2048,2,4,10]{3,2,1,0:T(4,128)} reshape(f32[8,20480]{1,0:T(8,128)S(1)} %reduce.3) | data formatting | bytes 1310720
  383.4 9.7 %fusion.64 = f32[80,2048]{1,0:T(8,128)S(1)} fusion(f32[80,1024]{1,0:T(8,128)S(1)} %get-tuple-element.9, f32[1024,2048]{1,0:T(8,128)S(1)} %fusion.375, f32[1024]{0:T(1024)S(1)} %bitcast.150, f32[1024]{0:T(1024)S(1)} %bitcast.151, f32[1024]{0:T(1024)S(1)} %bitcast.149, f32[2048]{0:T(1024)S(1)} %get-tuple-element.64, f32[2048]{0:T(1024)S(1)} %fusion.311, ...), kind=kOutput, calls=%fused_computation.66 | convolution fusion | flops 2044723200 | bytes 9408512 | tf_op jit(solution)/shard_map/dot_general | solution.py:89
  406.3 10.5 %fusion = f32[80,2048]{1,0:T(8,128)S(1)} fusion(f32[80,1024]{1,0:T(8,128)} %collective-permute-done.23, f32[1024,2048]{1,0:T(8,128)S(1)} %fusion.379, f32[1024]{0:T(1024)S(1)} %bitcast.156, f32[1024]{0:T(1024)S(1)} %bitcast.157, f32[1024]{0:T(1024)S(1)} %bitcast.155, f32[2048]{0:T(1024)S(1)} %get-tuple-element.64, f32[2048]{0:T(1024)S(1)} %fusion.311, ...), kind=kOutput, calls=%fused_computation.2 | convolution fusion | flops 2044723200 | bytes 9408512 | tf_op jit(solution)/shard_map/dot_general | solution.py:89
  426.1 9.7 %fusion.16 = f32[80,2048]{1,0:T(8,128)S(1)} fusion(f32[80,1024]{1,0:T(8,128)S(1)} %collective-permute-done.20, f32[1024,2048]{1,0:T(8,128)S(1)} %fusion.378, f32[1024]{0:T(1024)S(1)} %bitcast.177, f32[1024]{0:T(1024)S(1)} %bitcast.178, f32[1024]{0:T(1024)S(1)} %bitcast.176, f32[2048]{0:T(1024)S(1)} %get-tuple-element.64, f32[2048]{0:T(1024)S(1)} %fusion.311, ...), kind=kOutput, calls=%fused_computation.18 | convolution fusion | flops 2044723200 | bytes 9408512 | tf_op jit(solution)/shard_map/dot_general | solution.py:89
  442.8 9.8 %fusion.32 = f32[80,2048]{1,0:T(8,128)S(1)} fusion(f32[80,1024]{1,0:T(8,128)S(1)} %collective-permute-done.17, f32[1024,2048]{1,0:T(8,128)S(1)} %fusion.377, f32[1024]{0:T(1024)S(1)} %bitcast.174, f32[1024]{0:T(1024)S(1)} %bitcast.175, f32[1024]{0:T(1024)S(1)} %bitcast.173, f32[2048]{0:T(1024)S(1)} %get-tuple-element.64, f32[2048]{0:T(1024)S(1)} %fusion.311, ...), kind=kOutput, calls=%fused_computation.34 | convolution fusion | flops 2044723200 | bytes 9408512 | tf_op jit(solution)/shard_map/dot_general | solution.py:89
  459.8 9.7 %fusion.281 = f32[80,2048]{1,0:T(8,128)S(1)} fusion(f32[80,2048]{1,0:T(8,128)S(1)} %fusion, f32[80,2048]{1,0:T(8,128)S(1)} %fusion.16, f32[80,2048]{1,0:T(8,128)S(1)} %fusion.32, f32[80,2048]{1,0:T(8,128)S(1)} %fusion.64, f32[80,1024]{1,0:T(8,128)S(1)} %collective-permute-done.14, f32[1024,2048]{1,0:T(8,128)S(1)} %fusion.376, f32[1024]{0:T(1024)S(1)} %bitcast.168, ...), kind=kOutput, calls=%fused_computation.269 | convolution fusion | flops 2045378560 | bytes 12029952 | tf_op jit(solution)/shard_map/dot_general | solution.py:89
  470.1 16.3 %all_to_all.72 = f32[80,2,4,256]{3,2,1,0:T(4,128)S(1)} all-to-all(f32[80,2,4,256]{3,2,1,0:T(4,128)S(1)} %bitcast_add_fusion.1), channel_id=1, replica_groups=mesh['tile'=32,'ens'=8] {'ens'}, dimensions={0} | all-to-all | bytes 1310720 | tf_op jit(solution)/shard_map/all_to_all | solution.py:182
  (138 shorter events, 223.7 us)
Async XLA Ops:
  0.9 29.2 %collective-permute-start.13 = (f32[3,1024]{1,0:T(4,128)S(1)}, f32[3,1024]{1,0:T(4,128)S(1)}, u32[]{:S(2)}, u32[]{:S(2)}) collective-permute-start(f32[3,1024]{1,0:T(4,128)S(1)} %bitcast.143), channel_id=1, source_target_pairs={{16,0},{24,8},{32,16},{40,24},{48,32},{56,40},{64,48},{72,56},{80,... | collective-permute-start | bytes 36872 | tf_op jit(solution)/shard_map/ppermute | solution.py:35
  9.0 23.5 %collective-permute-start.10 = (f32[3,1024]{1,0:T(4,128)S(1)}, f32[3,1024]{1,0:T(4,128)S(1)}, u32[]{:S(2)}, u32[]{:S(2)}) collective-permute-start(f32[3,1024]{1,0:T(4,128)S(1)} %bitcast.144), channel_id=1, source_target_pairs={{0,16},{8,24},{16,32},{24,40},{32,48},{40,56},{48,64},{56,72},{64,... | collective-permute-start | bytes 36872 | tf_op jit(solution)/shard_map/ppermute | solution.py:35
  11.0 29.7 %collective-permute-start.7 = (f32[3,1024]{1,0:T(4,128)S(1)}, f32[3,1024]{1,0:T(4,128)S(1)}, u32[]{:S(2)}, u32[]{:S(2)}) collective-permute-start(f32[3,1024]{1,0:T(4,128)S(1)} %bitcast.145), channel_id=1, source_target_pairs={{8,0},{16,8},{24,16},{32,24},{40,32},{48,40},{56,48},{64,56},{72,6... | collective-permute-start | bytes 36872 | tf_op jit(solution)/shard_map/ppermute | solution.py:35
  17.5 25.2 %collective-permute-start.4 = (f32[3,1024]{1,0:T(4,128)S(1)}, f32[3,1024]{1,0:T(4,128)S(1)}, u32[]{:S(2)}, u32[]{:S(2)}) collective-permute-start(f32[3,1024]{1,0:T(4,128)S(1)} %bitcast.146), channel_id=1, source_target_pairs={{0,8},{8,16},{16,24},{24,32},{32,40},{40,48},{48,56},{56,64},{64,7... | collective-permute-start | bytes 36872 | tf_op jit(solution)/shard_map/ppermute | solution.py:35
  19.4 29.3 %collective-permute-start.25 = (f32[3,1024]{1,0:T(4,128)S(1)}, f32[3,1024]{1,0:T(4,128)S(1)}, u32[]{:S(2)}, u32[]{:S(2)}) collective-permute-start(f32[3,1024]{1,0:T(4,128)S(1)} %bitcast.139), channel_id=1, source_target_pairs={{16,0},{24,8},{32,16},{40,24},{48,32},{56,40},{64,48},{72,56},{80,... | collective-permute-start | bytes 36872 | tf_op jit(solution)/shard_map/ppermute | solution.py:35
  30.1 237.2 %collective-permute-start.22 = (f32[3,1024]{1,0:T(4,128)S(1)}, f32[3,1024]{1,0:T(4,128)S(1)}, u32[]{:S(2)}, u32[]{:S(2)}) collective-permute-start(f32[3,1024]{1,0:T(4,128)S(1)} %bitcast.140), channel_id=1, source_target_pairs={{0,16},{8,24},{16,32},{24,40},{32,48},{40,56},{48,64},{56,72},{64,... | collective-permute-start | bytes 36872 | tf_op jit(solution)/shard_map/ppermute | solution.py:35
  32.5 234.8 %collective-permute-start.19 = (f32[3,1024]{1,0:T(4,128)S(1)}, f32[3,1024]{1,0:T(4,128)S(1)}, u32[]{:S(2)}, u32[]{:S(2)}) collective-permute-start(f32[3,1024]{1,0:T(4,128)S(1)} %bitcast.141), channel_id=1, source_target_pairs={{8,0},{16,8},{24,16},{32,24},{40,32},{48,40},{56,48},{64,56},{72,6... | collective-permute-start | bytes 36872 | tf_op jit(solution)/shard_map/ppermute | solution.py:35
  40.7 226.6 %collective-permute-start.16 = (f32[3,1024]{1,0:T(4,128)S(1)}, f32[3,1024]{1,0:T(4,128)S(1)}, u32[]{:S(2)}, u32[]{:S(2)}) collective-permute-start(f32[3,1024]{1,0:T(4,128)S(1)} %bitcast.142), channel_id=1, source_target_pairs={{0,8},{8,16},{16,24},{24,32},{32,40},{40,48},{48,56},{56,64},{64,7... | collective-permute-start | bytes 36872 | tf_op jit(solution)/shard_map/ppermute | solution.py:35
  108.1 15.5 %all-to-all-start = ((f32[8,1,20480]{2,1,0:T(1,128)}), f32[8,1,20480]{2,1,0:T(1,128)S(1)}, u32[]{:S(2)}, u32[]{:S(2)}) async-start(f32[8,1,20480]{2,1,0:T(1,128)} %reshape.233), calls=%async_computation | async-start | bytes 1310720 | tf_op jit(solution)/shard_map/all_to_all | solution.py:164
  112.1 62.0 %collective-permute-start.11 = (f32[80,1024]{1,0:T(8,128)S(1)}, f32[80,1024]{1,0:T(8,128)S(1)}, u32[]{:S(2)}, u32[]{:S(2)}) collective-permute-start(f32[80,1024]{1,0:T(8,128)S(1)} %get-tuple-element.11), channel_id=1, source_target_pairs={{16,0},{24,8},{32,16},{40,24},{48,32},{56,40},{64,48},{72,56},{80,... | collective-permute-start | bytes 983048 | tf_op jit(solution)/shard_map/ppermute | solution.py:35
  114.0 51.2 %collective-permute-start.12 = (f32[80,1024]{1,0:T(8,128)S(1)}, f32[80,1024]{1,0:T(8,128)S(1)}, u32[]{:S(2)}, u32[]{:S(2)}) collective-permute-start(f32[80,1024]{1,0:T(8,128)S(1)} %get-tuple-element.10), channel_id=1, source_target_pairs={{16,0},{24,8},{32,16},{40,24},{48,32},{56,40},{64,48},{72,56},{80,... | collective-permute-start | bytes 983048 | tf_op jit(solution)/shard_map/ppermute | solution.py:35
  165.2 43.2 %collective-permute-start.8 = (f32[80,1024]{1,0:T(8,128)S(1)}, f32[80,1024]{1,0:T(8,128)S(1)}, u32[]{:S(2)}, u32[]{:S(2)}) collective-permute-start(f32[80,1024]{1,0:T(8,128)S(1)} %get-tuple-element.11), channel_id=1, source_target_pairs={{0,16},{8,24},{16,32},{24,40},{32,48},{40,56},{48,64},{56,72},{64,... | collective-permute-start | bytes 983048 | tf_op jit(solution)/shard_map/ppermute | solution.py:35
  174.1 25.1 %collective-permute-start.9 = (f32[80,1024]{1,0:T(8,128)S(1)}, f32[80,1024]{1,0:T(8,128)S(1)}, u32[]{:S(2)}, u32[]{:S(2)}) collective-permute-start(f32[80,1024]{1,0:T(8,128)S(1)} %get-tuple-element.10), channel_id=1, source_target_pairs={{0,16},{8,24},{16,32},{24,40},{32,48},{40,56},{48,64},{56,72},{64,... | collective-permute-start | bytes 983048 | tf_op jit(solution)/shard_map/ppermute | solution.py:35
  199.2 32.1 %collective-permute-start.5 = (f32[80,1024]{1,0:T(8,128)S(1)}, f32[80,1024]{1,0:T(8,128)S(1)}, u32[]{:S(2)}, u32[]{:S(2)}) collective-permute-start(f32[80,1024]{1,0:T(8,128)S(1)} %get-tuple-element.11), channel_id=1, source_target_pairs={{8,0},{16,8},{24,16},{32,24},{40,32},{48,40},{56,48},{64,56},{72,6... | collective-permute-start | bytes 983048 | tf_op jit(solution)/shard_map/ppermute | solution.py:35
  220.4 32.0 %collective-permute-start.2 = (f32[80,1024]{1,0:T(8,128)S(1)}, f32[80,1024]{1,0:T(8,128)S(1)}, u32[]{:S(2)}, u32[]{:S(2)}) collective-permute-start(f32[80,1024]{1,0:T(8,128)S(1)} %get-tuple-element.11), channel_id=1, source_target_pairs={{0,8},{8,16},{16,24},{24,32},{32,40},{40,48},{48,56},{56,64},{64,7... | collective-permute-start | bytes 983048 | tf_op jit(solution)/shard_map/ppermute | solution.py:35
  327.7 25.8 %all-to-all-start.2 = ((f32[8,1,20480]{2,1,0:T(1,128)}), f32[8,1,20480]{2,1,0:T(1,128)S(1)}, u32[]{:S(2)}, u32[]{:S(2)}) async-start(f32[8,1,20480]{2,1,0:T(1,128)} %reshape.235), calls=%async_computation.2 | async-start | bytes 1310720 | tf_op jit(solution)/shard_map/all_to_all | solution.py:164
  331.4 70.7 %collective-permute-start.23 = (f32[80,1024]{1,0:T(8,128)S(1)}, f32[80,1024]{1,0:T(8,128)}, u32[]{:S(2)}, u32[]{:S(2)}) collective-permute-start(f32[80,1024]{1,0:T(8,128)S(1)} %get-tuple-element.9), channel_id=1, source_target_pairs={{16,0},{24,8},{32,16},{40,24},{48,32},{56,40},{64,48},{72,56},{80,... | collective-permute-start | bytes 983048 | tf_op jit(solution)/shard_map/ppermute | solution.py:35
  335.0 91.1 %collective-permute-start.20 = (f32[80,1024]{1,0:T(8,128)S(1)}, f32[80,1024]{1,0:T(8,128)S(1)}, u32[]{:S(2)}, u32[]{:S(2)}) collective-permute-start(f32[80,1024]{1,0:T(8,128)S(1)} %get-tuple-element.9), channel_id=1, source_target_pairs={{0,16},{8,24},{16,32},{24,40},{32,48},{40,56},{48,64},{56,72},{64,... | collective-permute-start | bytes 983048 | tf_op jit(solution)/shard_map/ppermute | solution.py:35
  338.2 55.0 %collective-permute-start.24 = (f32[80,1024]{1,0:T(8,128)S(1)}, f32[80,1024]{1,0:T(8,128)S(1)}, u32[]{:S(2)}, u32[]{:S(2)}) collective-permute-start(f32[80,1024]{1,0:T(8,128)S(1)} %get-tuple-element.8), channel_id=1, source_target_pairs={{16,0},{24,8},{32,16},{40,24},{48,32},{56,40},{64,48},{72,56},{80,... | collective-permute-start | bytes 983048 | tf_op jit(solution)/shard_map/ppermute | solution.py:35
  343.9 73.0 %collective-permute-start.21 = (f32[80,1024]{1,0:T(8,128)S(1)}, f32[80,1024]{1,0:T(8,128)S(1)}, u32[]{:S(2)}, u32[]{:S(2)}) collective-permute-start(f32[80,1024]{1,0:T(8,128)S(1)} %get-tuple-element.8), channel_id=1, source_target_pairs={{0,16},{8,24},{16,32},{24,40},{32,48},{40,56},{48,64},{56,72},{64,... | collective-permute-start | bytes 983048 | tf_op jit(solution)/shard_map/ppermute | solution.py:35
  345.8 97.0 %collective-permute-start.17 = (f32[80,1024]{1,0:T(8,128)S(1)}, f32[80,1024]{1,0:T(8,128)S(1)}, u32[]{:S(2)}, u32[]{:S(2)}) collective-permute-start(f32[80,1024]{1,0:T(8,128)S(1)} %get-tuple-element.9), channel_id=1, source_target_pairs={{8,0},{16,8},{24,16},{32,24},{40,32},{48,40},{56,48},{64,56},{72,6... | collective-permute-start | bytes 983048 | tf_op jit(solution)/shard_map/ppermute | solution.py:35
  393.2 42.6 %collective-permute-start.18 = (f32[80,1024]{1,0:T(8,128)S(1)}, f32[80,1024]{1,0:T(8,128)S(1)}, u32[]{:S(2)}, u32[]{:S(2)}) collective-permute-start(f32[80,1024]{1,0:T(8,128)S(1)} %get-tuple-element.8), channel_id=1, source_target_pairs={{8,0},{16,8},{24,16},{32,24},{40,32},{48,40},{56,48},{64,56},{72,6... | collective-permute-start | bytes 983048 | tf_op jit(solution)/shard_map/ppermute | solution.py:35
  402.2 57.6 %collective-permute-start.14 = (f32[80,1024]{1,0:T(8,128)S(1)}, f32[80,1024]{1,0:T(8,128)S(1)}, u32[]{:S(2)}, u32[]{:S(2)}) collective-permute-start(f32[80,1024]{1,0:T(8,128)S(1)} %get-tuple-element.9), channel_id=1, source_target_pairs={{0,8},{8,16},{16,24},{24,32},{32,40},{40,48},{48,56},{56,64},{64,7... | collective-permute-start | bytes 983048 | tf_op jit(solution)/shard_map/ppermute | solution.py:35
  416.8 35.8 %collective-permute-start.15 = (f32[80,1024]{1,0:T(8,128)S(1)}, f32[80,1024]{1,0:T(8,128)S(1)}, u32[]{:S(2)}, u32[]{:S(2)}) collective-permute-start(f32[80,1024]{1,0:T(8,128)S(1)} %get-tuple-element.8), channel_id=1, source_target_pairs={{0,8},{8,16},{16,24},{24,32},{32,40},{40,48},{48,56},{56,64},{64,7... | collective-permute-start | bytes 983048 | tf_op jit(solution)/shard_map/ppermute | solution.py:35
  (10 other events, 173.4 us)
where the time goes:
time: 496 us; the launch traced here: 488 us
  matrix products  168 us (34%)
  local copies, waits for them, and re-layouts  114 us (23%)
  starting transfers between devices  105 us (21%)
  blocking collectives  43 us (9%)
  waiting for transfers between devices  40.2 us (8%)
  other arithmetic  15.9 us (3%)
    dot_general x10, matrix products, block_gain(): jnp.dot(obs_shift, gain_map, precision=PRECISE, preferred_element_type=jn...  97.6 us
    ppermute x24, starting transfers between devices, shifted(): lax.ppermute(value, axis, [(source, source + steps) for source in range(l...  86.5 us
    dot_general x10, matrix products, block_gain(): lax.dot_general(weight, states, (((0,), (0,)), ((), ())), precision=PRECI...  70 us
    unnamed x22, local copies, waits for them, and re-layouts  54.4 us
    all_gather x2, blocking collectives, on_device(): prior_obs = lax.all_gather(own_prior, 'ens', axis=0, tiled=True)  26.7 us
    all_to_all x3, local copies, waits for them, and re-layouts, on_device(): lax.all_to_all(columns, 'ens', split_axis=0, concat_axis=3, tiled=True)  17.7 us
    all_to_all x1, blocking collectives, on_device(): lax.all_to_all(columns, 'ens', split_axis=0, concat_axis=3, tiled=True)  16.3 us
    all_to_all x4, local copies, waits for them, and re-layouts, on_device(): lax.all_to_all(current_model_vector, 'ens', split_axis=3, concat_axis=0,...  13.7 us
  transfers between devices with their start and end apart: 29, of which 5 were waited for; matrix products, arithmetic and copies ran while one was open for 51% of the time, Pallas kernels for 0%

commit v1 on v0

v1 whole, which is shorter than its diff:
```python
import functools

import jax
import jax.numpy as jnp
from jax import lax
from jax.experimental import pallas as pl
from jax.experimental.pallas import tpu as pltpu
from jax.sharding import PartitionSpec as P

BATCHES = 2
REACH = 2
WINDOW = 2 * REACH + 1
SPREAD_RATE = 0.05
EPSILON = 1e-06
MESH = pl.DeviceIdType.MESH
VMEM = pltpu.VMEM
LANES = 128
BLOCK = 256
FORWARD_RIGHT = (2, 1, 3)
ORDER = (2, 1, 3, 0, 4)
F32 = jnp.float32
BF16 = jnp.bfloat16


def rdma(src, dst, send_sem, recv_sem, device):
    return pltpu.make_async_remote_copy(
        src_ref=src,
        dst_ref=dst,
        send_sem=send_sem,
        recv_sem=recv_sem,
        device_id=device,
        device_id_type=MESH,
    )


def greet(devices):
    barrier = pltpu.get_barrier_semaphore()
    for device in devices:
        pl.semaphore_signal(barrier, inc=1, device_id=device, device_id_type=MESH)
    pl.semaphore_wait(barrier, len(devices))


def split2(value):
    high = value.astype(BF16).astype(F32)
    return high, value - high


def exchange(gathered, send, recv, t, e, nt, ne, mid=None):
    right, left, opposite = lax.rem(e + 2, ne), lax.rem(e + ne - 2, ne), lax.rem(e + 4, ne)
    partner = e + 1 - 2 * lax.rem(e, 2)
    slots = [
        e,
        left,
        right,
        opposite,
        partner,
        lax.rem(partner + ne - 2, ne),
        lax.rem(partner + 2, ne),
        lax.rem(partner + 4, ne),
    ]
    started = []

    def go(k, rel, target_k, target_rel, device):
        copy = rdma(
            gathered.at[k, slots[rel]],
            gathered.at[target_k, slots[rel]],
            send.at[len(started)],
            recv.at[target_k, target_rel],
            device,
        )
        copy.start()
        started.append(copy)

    def arrive(k, rel):
        rdma(
            gathered.at[k, slots[rel]],
            gathered.at[k, slots[rel]],
            send.at[0],
            recv.at[k, rel],
            (t, partner),
        ).wait_recv()

    for offset in (1, -1, 2, -2):
        go(REACH, 0, REACH - offset, 0, (lax.rem(t + nt + offset, nt), e))
    if mid is not None:
        mid()
    for k in ORDER:
        if k != REACH:
            arrive(k, 0)
        go(k, 0, k, 1, (t, right))
        go(k, 0, k, 2, (t, left))
        go(k, 0, k, 4, (t, partner))
    for k in ORDER:
        arrive(k, 1)
        if k in FORWARD_RIGHT:
            go(k, 1, k, 3, (t, right))
        go(k, 1, k, 5, (t, partner))
        arrive(k, 2)
        if k not in FORWARD_RIGHT:
            go(k, 2, k, 3, (t, left))
        go(k, 2, k, 6, (t, partner))
    for k in ORDER:
        arrive(k, 3)
        go(k, 3, k, 7, (t, partner))
    for k in ORDER:
        for rel in (4, 5, 6, 7):
            arrive(k, rel)
    for copy in started:
        copy.wait_send()


EXCHANGE_SENDS = 4 + 3 * WINDOW + 3 * WINDOW + WINDOW


def tile_peers(t, e, nt):
    return [(lax.rem(t + nt + offset, nt), e) for offset in (1, -1, 2, -2)]


def ens_peers(t, e, ne):
    return [(t, lax.rem(e + d, ne)) for d in range(1, ne)]


def forecast_kernel(
    nt, ne,
    x, u, loc, cnt, val, err,
    gathered, cols, second, meta,
    hs, hr, tmp, ub, bg, parts, sb, rb,
    halo_s, halo_r, meta_s, meta_r, bulk_s, bulk_r, small_s, small_r, ex_s, ex_r, own_sem,
):
    t, e = lax.axis_index("tile"), lax.axis_index("ens")
    per, levels, rows, width = x.shape
    lr = levels * rows
    col_count = width // ne
    slots = loc.shape[2]

    def fill(m, carry):
        for l in range(levels):
            hs[0, m, l : l + 1, :] = x[m, l, 0:1, :]
            hs[1, m, l : l + 1, :] = x[m, l, rows - 1 : rows, :]
        return carry

    lax.fori_loop(0, per, fill, 0)
    slot_index = lax.broadcasted_iota(jnp.int32, (1, slots), 1)
    for b in range(BATCHES):
        for i in range(3):
            meta[REACH, b, i : i + 1, :] = loc[i, b : b + 1, :].astype(F32)
        meta[REACH, b, 3:4, :] = val[b : b + 1, :]
        meta[REACH, b, 4:5, :] = err[b : b + 1, :]
        meta[REACH, b, 5:6, :] = (slot_index < cnt[b : b + 1, 0:1]).astype(F32)
        meta[REACH, b, 6:8, :] = jnp.zeros((2, slots), F32)
    greet(tile_peers(t, e, nt) + ens_peers(t, e, ne))
    up_tile, down_tile = lax.rem(t + nt - 1, nt), lax.rem(t + 1, nt)
    halos = [
        rdma(hs.at[1], hr.at[0], halo_s.at[0], halo_r.at[0], (down_tile, e)),
        rdma(hs.at[0], hr.at[1], halo_s.at[1], halo_r.at[1], (up_tile, e)),
    ]
    for copy in halos:
        copy.start()
    metas = []
    for i, offset in enumerate((1, -1, 2, -2)):
        copy = rdma(
            meta.at[REACH],
            meta.at[REACH - offset],
            meta_s.at[i],
            meta_r.at[i],
            (lax.rem(t + nt + offset, nt), e),
        )
        copy.start()
        metas.append(copy)
    for a in range(2):
        for l in range(levels):
            ub[a, l * rows : (l + 1) * rows, :] = u[a, l]
    for copy in halos:
        copy.wait_recv()
    has_up = jnp.where(t > 0, 1.0, 0.0).astype(F32)
    has_down = jnp.where(t < nt - 1, 1.0, 0.0).astype(F32)

    def step(m, carry):
        for l in range(levels):
            tmp[l * rows : (l + 1) * rows, :] = x[m, l]
        c = tmp[...]
        above = hr[0, m] * has_up
        below = hr[1, m] * has_down
        row = lax.broadcasted_iota(jnp.int32, (lr, width), 0)
        col = lax.broadcasted_iota(jnp.int32, (lr, width), 1)
        up = pltpu.roll(c, 1, 0)
        down = pltpu.roll(c, lr - 1, 0)
        for l in range(levels):
            up = jnp.where(row == l * rows, above[l : l + 1], up)
            down = jnp.where(row == l * rows + rows - 1, below[l : l + 1], down)
        west = jnp.where(col == 0, 0.0, pltpu.roll(c, 1, 1))
        east = jnp.where(col == width - 1, 0.0, pltpu.roll(c, width - 1, 1))
        wr, wc = ub[0], ub[1]
        tendency = (
            jnp.maximum(wr, 0.0) * (c - up)
            + jnp.minimum(wr, 0.0) * (down - c)
            + jnp.maximum(wc, 0.0) * (c - west)
            + jnp.minimum(wc, 0.0) * (east - c)
        )
        ahead = c - tendency + SPREAD_RATE * (up + down + west + east - 4.0 * c)
        for i in range(width // LANES):
            bg[i, m] = ahead[:, i * LANES : (i + 1) * LANES]
        return carry

    lax.fori_loop(0, per, step, 0)

    pieces = col_count // LANES

    def block_of(device):
        return pl.ds(device * pieces, pieces)

    bulks = []

    def send_bulk(d):
        peer = lax.rem(e + d, ne)
        copy = rdma(
            bg.at[block_of(peer)],
            cols.at[:, pl.ds(e * per, per)],
            bulk_s.at[d],
            bulk_r.at[d],
            (t, peer),
        )
        copy.start()
        bulks.append(copy)

    own = pltpu.make_async_copy(bg.at[block_of(e)], cols.at[:, pl.ds(e * per, per)], own_sem)
    own.start()
    for d in (1, 2, ne - 1, ne - 2):
        send_bulk(d)

    def split(kk, carry):
        f = jnp.concatenate(
            [bg[2 * kk].reshape(per * lr, LANES), bg[2 * kk + 1].reshape(per * lr, LANES)], axis=1
        )
        high, rest = split2(f)
        middle, low = split2(rest)
        parts[kk] = jnp.concatenate([high, middle, low], axis=0).astype(BF16)
        return carry

    lax.fori_loop(0, width // BLOCK, split, 0)
    held = per * lr
    for b in range(BATCHES):

        def pick(j, carry):
            here = pl.ds(pl.multiple_of(j * BLOCK, BLOCK), BLOCK)
            place = loc[2, b : b + 1, here] * rows + (loc[0, b : b + 1, here] - t * rows)
            column = loc[1, b : b + 1, here]
            down = lax.broadcasted_iota(jnp.int32, (BLOCK, BLOCK), 0)
            total = jnp.zeros((3 * held, BLOCK), F32)
            for kk in range(width // BLOCK):
                hot = jnp.where(down == column - kk * BLOCK, 1.0, 0.0).astype(BF16)
                total += jnp.dot(parts[kk], hot, preferred_element_type=F32)
            value = total[0:held] + total[held : 2 * held] + total[2 * held :]
            mine = lax.broadcasted_iota(jnp.int32, (lr, BLOCK), 0) == place
            value = jnp.where(mine[None], value.reshape(per, lr, BLOCK), 0.0)
            value = jnp.sum(value, axis=1)
            for half in range(BLOCK // LANES):
                sb[j * (BLOCK // LANES) + half, b, 0:per, :] = value[
                    :, half * LANES : (half + 1) * LANES
                ]
            return carry

        lax.fori_loop(0, slots // BLOCK, pick, 0)

    smalls = []
    for d in (4, 3, 5, 2, 6, 1, 7):
        peer = lax.rem(e + d, ne)
        copy = rdma(sb.at[peer], rb.at[e], small_s.at[d], small_r.at[d], (t, peer))
        copy.start()
        smalls.append(copy)
    for d in (4, 3, 5):
        send_bulk(d)
    rb[e] = sb[e]
    for d in range(1, ne):
        source = lax.rem(e + ne - d, ne)
        rdma(
            sb.at[source], rb.at[source], small_s.at[d], small_r.at[d], (t, source)
        ).wait_recv()
    for s in range(ne):
        gathered[REACH, e, s * per : (s + 1) * per, :] = rb[s, 0, 0:per, :]
        second[s * per : (s + 1) * per, :] = rb[s, 1, 0:per, :]
    exchange(gathered, ex_s, ex_r, t, e, nt, ne)
    own.wait()
    for d in range(1, ne):
        source = lax.rem(e + ne - d, ne)
        rdma(
            bg.at[block_of(source)],
            cols.at[:, pl.ds(source * per, per)],
            bulk_s.at[d],
            bulk_r.at[d],
            (t, source),
        ).wait_recv()
    for i, offset in enumerate((1, -1, 2, -2)):
        rdma(
            meta.at[REACH],
            meta.at[REACH - offset],
            meta_s.at[i],
            meta_r.at[i],
            (up_tile, e),
        ).wait_recv()
    for copy in halos + metas + bulks + smalls:
        copy.wait_send()


def gather_kernel(nt, ne, prior, gathered, ex_s, ex_r):
    t, e = lax.axis_index("tile"), lax.axis_index("ens")
    gathered[REACH, e] = prior[...]
    partner = e + 1 - 2 * lax.rem(e, 2)
    ring = [(t, lax.rem(e + 2, ne)), (t, lax.rem(e + ne - 2, ne)), (t, partner)]
    greet(tile_peers(t, e, nt) + ring)
    exchange(gathered, ex_s, ex_r, t, e, nt, ne)


def spread_kernel(nt, ne, cols, out, grid, send, recv):
    t, e = lax.axis_index("tile"), lax.axis_index("ens")
    per, levels, rows, width = out.shape
    pieces = width // ne // LANES
    greet(ens_peers(t, e, ne))

    def block_of(device):
        return pl.ds(device * pieces, pieces)

    copies = []
    for d in (4, 3, 5, 2, 6, 1, 7):
        peer = lax.rem(e + d, ne)
        copy = rdma(
            cols.at[:, pl.ds(peer * per, per)],
            grid.at[block_of(e)],
            send.at[d],
            recv.at[d],
            (t, peer),
        )
        copy.start()
        copies.append(copy)
    own = pltpu.make_async_copy(
        cols.at[:, pl.ds(e * per, per)], grid.at[block_of(e)], send.at[0]
    )
    own.start()
    own.wait()
    for d in range(1, ne):
        source = lax.rem(e + ne - d, ne)
        rdma(
            cols.at[:, pl.ds(source * per, per)],
            grid.at[block_of(source)],
            send.at[d],
            recv.at[d],
            (t, source),
        ).wait_recv()

    def put(m, carry):
        for l in range(levels):
            for i in range(width // LANES):
                out[m, l, :, i * LANES : (i + 1) * LANES] = grid[i, m, l * rows : (l + 1) * rows, :]
        return carry

    lax.fori_loop(0, per, put, 0)
    for copy in copies:
        copy.wait_send()


def update_kernel(nt, ne, batch, look_ahead, *refs):
    if look_ahead:
        gathered, meta, cols, second, out, prior, weights, shifts, states, total, ahead = refs
    else:
        gathered, meta, cols, out, weights, shifts, states, total = refs
    t, e = lax.axis_index("tile"), lax.axis_index("ens")
    members = gathered.shape[2]
    slices = gathered.shape[1]
    halves = cols.shape[0]
    lr = cols.shape[1] // members
    levels = 2
    rows = lr // levels
    width = halves * LANES
    col_total = width * ne
    inverse_col = 1.0 / float(col_total // 2)
    inverse_row = 1.0 / float(REACH * rows)

    def blocks(k):
        live = jnp.sum(meta[k, batch, 5:6, :])
        return (live.astype(jnp.int32) + (BLOCK - 1)) // BLOCK

    def prepare(k, carry):
        def piece(s, inner):
            here = pl.ds(pl.multiple_of(s * LANES, LANES), LANES)
            p = gathered[k, s]
            lev = meta[k, batch, 2:3, here]
            value = meta[k, batch, 3:4, here]
            error = meta[k, batch, 4:5, here]
            live = meta[k, batch, 5:6, here]
            average = jnp.sum(p, axis=0, keepdims=True) / members
            deviation = p - average
            variance = (
                jnp.sum(deviation * deviation, axis=0, keepdims=True) / (members - 1) + EPSILON
            )
            combined = variance + error
            shrink = jnp.sqrt(error / combined)
            mean_post = (error * average + variance * value) / combined
            shift = live * ((shrink - 1.0) * deviation + (mean_post - average))
            weight = deviation * (live / ((members - 1) * variance))
            high, low = split2(weight)
            for l in range(levels):
                factor = jnp.where(lev == float(l), 1.0, 0.5)
                scaled = (high * factor).astype(BF16)
                weights[k, l, 0:members, here] = scaled
                weights[k, l, members : 2 * members, here] = scaled
                weights[k, l, 2 * members : 3 * members, here] = (low * factor).astype(BF16)
            both = jnp.concatenate(split2(shift), axis=0)
            shifts[k, here, :] = both.T.astype(BF16)
            return inner

        lax.fori_loop(0, blocks(k) * (BLOCK // LANES), piece, 0)
        return carry

    lax.fori_loop(0, WINDOW, prepare, 0)

    def cell_major(value):
        high, low = split2(value)
        return jnp.concatenate([high, low, high], axis=0).T.astype(BF16)

    def member_major(value):
        turned = value.T
        return turned[0:members] + turned[members : 2 * members]

    for i in range(lr):
        here = pl.ds(i, members, stride=lr)
        states[i] = cell_major(jnp.concatenate([cols[h, here, :] for h in range(halves)], axis=1))
    total[...] = jnp.zeros_like(total)

    def apply(gain, k, here):
        high = gain.astype(BF16)
        low = (gain - high.astype(F32)).astype(BF16)
        right = shifts[k, here, :]
        return jnp.dot(high, right, preferred_element_type=F32) + jnp.dot(
            low, right, preferred_element_type=F32
        )

    if look_ahead:
        mine = pl.ds(pl.multiple_of(e * LANES, LANES), LANES)
        places = meta[REACH, batch + 1, :, mine].T
        cell_row, cell_col, cell_lev = places[:, 0:1], places[:, 1:2], places[:, 2:3]
        x2 = cell_major(second[...])
        ahead[...] = jnp.zeros_like(ahead)

        def look(k, carry):
            def block(j, inner):
                here = pl.ds(pl.multiple_of(j * BLOCK, BLOCK), BLOCK)
                row_gap = (cell_row - meta[k, batch, 0:1, here]) * inverse_row
                col_gap = (cell_col - meta[k, batch, 1:2, here]) * inverse_col
                close = jnp.maximum(1.0 - row_gap * row_gap - col_gap * col_gap, 0.0)
                first = jnp.dot(x2, weights[k, 0, :, here], preferred_element_type=F32)
                other = jnp.dot(x2, weights[k, 1, :, here], preferred_element_type=F32)
                gain = jnp.where(cell_lev == 0.0, first, other) * (close * close)
                ahead[...] += apply(gain, k, here)
                return inner

            lax.fori_loop(0, blocks(k), block, 0)
            return carry

        lax.fori_loop(0, WINDOW, look, 0)
        prior[...] = second[...] + member_major(ahead[...])

    cell_col = (lax.broadcasted_iota(jnp.int32, (width, BLOCK), 0) + e * width).astype(
        F32
    ) * inverse_col
    first_row = (t * rows).astype(F32)

    def main(k, carry):
        def block(j, inner):
            here = pl.ds(pl.multiple_of(j * BLOCK, BLOCK), BLOCK)
            col_gap = cell_col - meta[k, batch, 1:2, here] * inverse_col
            col_part = col_gap * col_gap
            obs_row = meta[k, batch, 0:1, here]
            for r in range(rows):
                row_gap = (first_row + float(r) - obs_row) * inverse_row
                close = jnp.maximum((1.0 - row_gap * row_gap) - col_part, 0.0)
                close = close * close
                for l in range(levels):
                    i = l * rows + r
                    covariance = jnp.dot(
                        states[i], weights[k, l, :, here], preferred_element_type=F32
                    )
                    total[i] += apply(covariance * close, k, here)
            return inner

        lax.fori_loop(0, blocks(k), block, 0)
        return carry

    lax.fori_loop(0, WINDOW, main, 0)
    for i in range(lr):
        here = pl.ds(i, members, stride=lr)
        change = member_major(total[i])
        for h in range(halves):
            out[h, here, :] = cols[h, here, :] + change[:, h * LANES : (h + 1) * LANES]


def on_device(nt, ne, x, u, loc, cnt, val, err):
    per, levels, rows, width = x.shape
    lr = levels * rows
    members = per * ne
    slots = val.shape[1]
    col_count = width // ne
    vmem = pl.BlockSpec(memory_space=VMEM)
    dma = pltpu.SemaphoreType.DMA
    window = jax.ShapeDtypeStruct((WINDOW, ne, members, LANES), F32)
    pieces = col_count // LANES
    flat = jax.ShapeDtypeStruct((pieces, members * lr, LANES), F32)
    gathered, cols, second, meta = pl.pallas_call(
        functools.partial(forecast_kernel, nt, ne),
        out_shape=[
            window,
            jax.ShapeDtypeStruct((pieces, members, lr, LANES), F32),
            jax.ShapeDtypeStruct((members, LANES), F32),
            jax.ShapeDtypeStruct((WINDOW, BATCHES, 8, slots), F32),
        ],
        in_specs=[vmem] * 6,
        out_specs=[vmem] * 4,
        scratch_shapes=[
            VMEM((2, per, levels, width), F32),
            VMEM((2, per, levels, width), F32),
            VMEM((lr, width), F32),
            VMEM((2, lr, width), F32),
            VMEM((width // LANES, per, lr, LANES), F32),
            VMEM((width // BLOCK, 3 * per * lr, BLOCK), BF16),
            VMEM((ne, BATCHES, 16, LANES), F32),
            VMEM((ne, BATCHES, 16, LANES), F32),
            dma((2,)),
            dma((2,)),
            dma((4,)),
            dma((4,)),
            dma((ne,)),
            dma((ne,)),
            dma((ne,)),
            dma((ne,)),
            dma((EXCHANGE_SENDS,)),
            dma((WINDOW, ne)),
            dma,
        ],
        compiler_params=pltpu.CompilerParams(collective_id=0, has_side_effects=True),
        name="forecast",
    )(x, u, loc, cnt, val, err)
    cols = cols.reshape(flat.shape)
    work = [
        VMEM((WINDOW, levels, 3 * members, slots), BF16),
        VMEM((WINDOW, slots, 2 * members), BF16),
        VMEM((lr, col_count, 3 * members), BF16),
        VMEM((lr, col_count, 2 * members), F32),
    ]
    cols, prior = pl.pallas_call(
        functools.partial(update_kernel, nt, ne, 0, True),
        out_shape=[flat, jax.ShapeDtypeStruct((members, LANES), F32)],
        in_specs=[vmem] * 4,
        out_specs=[vmem] * 2,
        scratch_shapes=work + [VMEM((LANES, 2 * members), F32)],
        name="first_update",
    )(gathered, meta, cols, second)
    gathered = pl.pallas_call(
        functools.partial(gather_kernel, nt, ne),
        out_shape=window,
        in_specs=[vmem],
        out_specs=vmem,
        scratch_shapes=[dma((EXCHANGE_SENDS,)), dma((WINDOW, ne))],
        compiler_params=pltpu.CompilerParams(collective_id=1, has_side_effects=True),
        name="gather",
    )(prior)
    cols = pl.pallas_call(
        functools.partial(update_kernel, nt, ne, 1, False),
        out_shape=flat,
        in_specs=[vmem] * 3,
        out_specs=vmem,
        scratch_shapes=work,
        name="second_update",
    )(gathered, meta, cols)
    return pl.pallas_call(
        functools.partial(spread_kernel, nt, ne),
        out_shape=jax.ShapeDtypeStruct(x.shape, F32),
        in_specs=[vmem],
        out_specs=vmem,
        scratch_shapes=[VMEM((width // LANES, per, lr, LANES), F32), dma((ne,)), dma((ne,))],
        compiler_params=pltpu.CompilerParams(collective_id=2, has_side_effects=True),
        name="spread",
    )(cols.reshape(pieces, members, lr, LANES))


def solution(mesh):
    in_specs = (
        P("ens", None, "tile", None),
        P(None, None, "tile", None),
        P(None, None, "tile"),
        P(None, "tile"),
        P(None, "tile"),
        P(None, "tile"),
    )
    out_specs = P("ens", None, "tile", None)
    body = functools.partial(on_device, mesh.shape["tile"], mesh.shape["ens"])
    return jax.shard_map(body, mesh=mesh, in_specs=in_specs, out_specs=out_specs, check_vma=False)
```

time: 496 us -> 151 us (0.30)
  the two profiles are of different devices: /device:TPU:2 before, /device:TPU:1 now
where the time goes in v1:
time: 151 us
  Pallas kernels  148 us (98%)
  local copies, waits for them, and re-layouts  3.28 us (2%)
    pallas_call x1, Pallas kernels, on_device(): pl.pallas_call(functools.partial(forecast_kernel, nt, ne), out_shape=[win...  46.7 us
    pallas_call x1, Pallas kernels, on_device(): pl.pallas_call(functools.partial(update_kernel, nt, ne, 0, True), out_sha...  40.4 us
    pallas_call x1, Pallas kernels, on_device(): pl.pallas_call(functools.partial(update_kernel, nt, ne, 1, False), out_sh...  25.4 us
    pallas_call x1, Pallas kernels, on_device(): pl.pallas_call(functools.partial(gather_kernel, nt, ne), out_shape=window...  21.2 us
    pallas_call x1, Pallas kernels, on_device(): pl.pallas_call(functools.partial(spread_kernel, nt, ne), out_shape=jax.Sh...  14.1 us
    unnamed x2, local copies, waits for them, and re-layouts  3.28 us

profile of v1, /device:TPU:1, one launch (start us, length us, event | category | flops | bytes accessed | tf_op | source)
XLA Modules:
  0.0 151.1 jit_solution(7767885831830160761)
XLA Ops:
  0.0 1.3 copy.7.cnt
  1.3 46.7 %forecast.1 = (f32[5,8,80,128]{3,2,1,0:T(8,128)}, f32[2,80,8,128]{3,2,1,0:T(8,128)}, f32[80,128]{1,0:T(8,128)}, f32[5,2,8,1024]{3,2,1,0:T(8,128)}) custom-call(f32[10,2,4,2048]{3,2,1,0:T(4,128)} %x.1, f32[2,2,4,2048]{3,2,1,0:T(4,128)} %u.1, s32[3,2,1024]{2,1,0:T(2,128)} %loc.1, s32[2,1]{1,0:T(2,128)} %copy.7.cnt, f32[2,1024]{1,0:T(2,128)} %val.1, f32[2,1024]{1,0:T(2,128)} %err.1), custom_call_target="tpu_custom_call" | custom-call | tf_op jit(solution)/shard_map/forecast/pallas_call | solution.py:507
  48.0 40.4 %first_update.1 = (f32[2,640,128]{2,1,0:T(8,128)}, f32[80,128]{1,0:T(8,128)}) custom-call(f32[5,8,80,128]{3,2,1,0:T(8,128)} %get-tuple-element.11.refs_0_, f32[5,2,8,1024]{3,2,1,0:T(8,128)} %get-tuple-element.12.refs_1_, f32[2,640,128]{2,1,0:T(8,128)} %bitcast.3, f32[80,128]{1,0:T(8,128)} %get-tuple-element.14.refs_3_), custom_call_target="tpu_custom_call" | custom-call | tf_op jit(solution)/shard_map/first_update/pallas_call | solution.py:548
  88.4 21.2 %gather.1.refs_0_ = f32[5,8,80,128]{3,2,1,0:T(8,128)} custom-call(f32[80,128]{1,0:T(8,128)} %get-tuple-element.15.prior), custom_call_target="tpu_custom_call" | custom-call | tf_op jit(solution)/shard_map/gather/pallas_call | solution.py:556
  109.6 25.4 %second_update.1 = f32[2,640,128]{2,1,0:T(8,128)} custom-call(f32[5,8,80,128]{3,2,1,0:T(8,128)} %gather.1.refs_0_, f32[5,2,8,1024]{3,2,1,0:T(8,128)} %get-tuple-element.12.refs_1_, f32[2,640,128]{2,1,0:T(8,128)} %get-tuple-element.16.refs_2_), custom_call_target="tpu_custom_call" | custom-call | tf_op jit(solution)/shard_map/second_update/pallas_call | solution.py:565
  135.0 14.1 %spread.1 = f32[10,2,4,2048]{3,2,1,0:T(4,128)} custom-call(f32[2,80,8,128]{3,2,1,0:T(8,128)} %bitcast.2), custom_call_target="tpu_custom_call" | custom-call | tf_op jit(solution)/shard_map/spread/pallas_call | solution.py:573
  149.2 2.0 %copy.9 = f32[10,2,4,2048]{3,2,1,0:T(4,128)} copy(f32[10,2,4,2048]{3,2,1,0:T(4,128)} %spread.1) | data formatting | bytes 1310720

commit v2 on v1

--- a/solution.py
+++ b/solution.py
@@ -146,7 +146,7 @@
             meta[REACH, b, i : i + 1, :] = loc[i, b : b + 1, :].astype(F32)
         meta[REACH, b, 3:4, :] = val[b : b + 1, :]
         meta[REACH, b, 4:5, :] = err[b : b + 1, :]
-        meta[REACH, b, 5:6, :] = (slot_index < cnt[b : b + 1, 0:1]).astype(F32)
+        meta[REACH, b, 5:6, :] = (slot_index < cnt[0:1, b : b + 1]).astype(F32)
         meta[REACH, b, 6:8, :] = jnp.zeros((2, slots), F32)
     greet(tile_peers(t, e, nt) + ens_peers(t, e, ne))
     up_tile, down_tile = lax.rem(t + nt - 1, nt), lax.rem(t + 1, nt)
@@ -360,9 +360,9 @@
 
 def update_kernel(nt, ne, batch, look_ahead, *refs):
     if look_ahead:
-        gathered, meta, cols, second, out, prior, weights, shifts, states, total, ahead = refs
+        gathered, meta, cols, second, out, prior, weights, shifts, states, total, closes, gains, ahead = refs
     else:
-        gathered, meta, cols, out, weights, shifts, states, total = refs
+        gathered, meta, cols, out, weights, shifts, states, total, closes, gains = refs
     t, e = lax.axis_index("tile"), lax.axis_index("ens")
     members = gathered.shape[2]
     slices = gathered.shape[1]
@@ -371,6 +371,7 @@
     levels = 2
     rows = lr // levels
     width = halves * LANES
+    span = rows * width
     col_total = width * ne
     inverse_col = 1.0 / float(col_total // 2)
     inverse_row = 1.0 / float(REACH * rows)
@@ -381,8 +382,8 @@
 
     def prepare(k, carry):
         def piece(s, inner):
-            here = pl.ds(pl.multiple_of(s * LANES, LANES), LANES)
-            p = gathered[k, s]
+            here = pl.ds(pl.multiple_of(s * BLOCK, BLOCK), BLOCK)
+            p = jnp.concatenate([gathered[k, 2 * s], gathered[k, 2 * s + 1]], axis=1)
             lev = meta[k, batch, 2:3, here]
             value = meta[k, batch, 3:4, here]
             error = meta[k, batch, 4:5, here]
@@ -408,7 +409,7 @@
             shifts[k, here, :] = both.T.astype(BF16)
             return inner
 
-        lax.fori_loop(0, blocks(k) * (BLOCK // LANES), piece, 0)
+        lax.fori_loop(0, blocks(k), piece, 0)
         return carry
 
     lax.fori_loop(0, WINDOW, prepare, 0)
@@ -423,7 +424,7 @@
 
     for i in range(lr):
         here = pl.ds(i, members, stride=lr)
-        states[i] = cell_major(jnp.concatenate([cols[h, here, :] for h in range(halves)], axis=1))
+        states[i // rows, i % rows * width : (i % rows + 1) * width, :] = cell_major(jnp.concatenate([cols[h, here, :] for h in range(halves)], axis=1))
     total[...] = jnp.zeros_like(total)
 
     def apply(gain, k, here):
@@ -473,13 +474,16 @@
             for r in range(rows):
                 row_gap = (first_row + float(r) - obs_row) * inverse_row
                 close = jnp.maximum((1.0 - row_gap * row_gap) - col_part, 0.0)
-                close = close * close
-                for l in range(levels):
-                    i = l * rows + r
-                    covariance = jnp.dot(
-                        states[i], weights[k, l, :, here], preferred_element_type=F32
-                    )
-                    total[i] += apply(covariance * close, k, here)
+                closes[r * width : (r + 1) * width, :] = close * close
+            for l in range(levels):
+                covariance = jnp.dot(states[l], weights[k, l, :, here], preferred_element_type=F32)
+                gain = covariance * closes[...]
+                high = gain.astype(BF16)
+                low = (gain - high.astype(F32)).astype(BF16)
+                gains[l * span : (l + 1) * span, :] = jnp.concatenate([high, low], axis=1)
+            right = shifts[k, here, :]
+            right = jnp.concatenate([right, right], axis=0)
+            total[...] += jnp.dot(gains[...], right, preferred_element_type=F32)
             return inner
 
         lax.fori_loop(0, blocks(k), block, 0)
@@ -488,7 +492,7 @@
     lax.fori_loop(0, WINDOW, main, 0)
     for i in range(lr):
         here = pl.ds(i, members, stride=lr)
-        change = member_major(total[i])
+        change = member_major(total[i * width : (i + 1) * width, :])
         for h in range(halves):
             out[h, here, :] = cols[h, here, :] + change[:, h * LANES : (h + 1) * LANES]
 
@@ -537,13 +541,15 @@
         ],
         compiler_params=pltpu.CompilerParams(collective_id=0, has_side_effects=True),
         name="forecast",
-    )(x, u, loc, cnt, val, err)
+    )(x, u, loc, cnt.T, val, err)
     cols = cols.reshape(flat.shape)
     work = [
         VMEM((WINDOW, levels, 3 * members, slots), BF16),
         VMEM((WINDOW, slots, 2 * members), BF16),
-        VMEM((lr, col_count, 3 * members), BF16),
-        VMEM((lr, col_count, 2 * members), F32),
+        VMEM((levels, rows * col_count, 3 * members), BF16),
+        VMEM((lr * col_count, 2 * members), F32),
+        VMEM((rows * col_count, BLOCK), F32),
+        VMEM((lr * col_count, 2 * BLOCK), BF16),
     ]
     cols, prior = pl.pallas_call(
         functools.partial(update_kernel, nt, ne, 0, True),

time: 151 us -> 136 us (0.901)
  Pallas kernels: 148 us -> 133 us
    pallas_call x1, Pallas kernels: 40.4 us -> 32.1 us  [on_device(): pl.pallas_call(functools.partial(update_kernel, nt, ne, 0, True), out_sha...]
    pallas_call x1, Pallas kernels: 25.4 us -> 19.5 us  [on_device(): pl.pallas_call(functools.partial(update_kernel, nt, ne, 1, False), out_sh...]
    unnamed x2 -> x1, local copies, waits for them, and re-layouts: 3.28 us -> 1.99 us
where the time goes in v2:
time: 136 us; the launch traced here: 135 us
  Pallas kernels  133 us (98%)
  local copies, waits for them, and re-layouts  1.99 us (1%)
    pallas_call x1, Pallas kernels, on_device(): pl.pallas_call(functools.partial(forecast_kernel, nt, ne), out_shape=[win...  46.7 us
    pallas_call x1, Pallas kernels, on_device(): pl.pallas_call(functools.partial(update_kernel, nt, ne, 0, True), out_sha...  32.1 us
    pallas_call x1, Pallas kernels, on_device(): pl.pallas_call(functools.partial(gather_kernel, nt, ne), out_shape=window...  21.3 us
    pallas_call x1, Pallas kernels, on_device(): pl.pallas_call(functools.partial(update_kernel, nt, ne, 1, False), out_sh...  19.5 us
    pallas_call x1, Pallas kernels, on_device(): pl.pallas_call(functools.partial(spread_kernel, nt, ne), out_shape=jax.Sh...  13.8 us

profile of v2, /device:TPU:1, one launch (start us, length us, event | category | flops | bytes accessed | tf_op | source)
XLA Modules:
  0.0 135.5 jit_solution(9797250811143346108)
XLA Ops:
  0.0 46.7 %forecast.1 = (f32[5,8,80,128]{3,2,1,0:T(8,128)}, f32[2,80,8,128]{3,2,1,0:T(8,128)}, f32[80,128]{1,0:T(8,128)}, f32[5,2,8,1024]{3,2,1,0:T(8,128)}) custom-call(f32[10,2,4,2048]{3,2,1,0:T(4,128)} %x.1, f32[2,2,4,2048]{3,2,1,0:T(4,128)} %u.1, s32[3,2,1024]{2,1,0:T(2,128)} %loc.1, s32[1,2]{1,0:T(1,128)} %bitcast.5, f32[2,1024]{1,0:T(2,128)} %val.1, f32[2,1024]{1,0:T(2,128)} %err.1), custom_call_target="tpu_custom_call" | custom-call | tf_op jit(solution)/shard_map/forecast/pallas_call | solution.py:511
  46.7 32.1 %first_update.1 = (f32[2,640,128]{2,1,0:T(8,128)}, f32[80,128]{1,0:T(8,128)}) custom-call(f32[5,8,80,128]{3,2,1,0:T(8,128)} %get-tuple-element.11.refs_0_, f32[5,2,8,1024]{3,2,1,0:T(8,128)} %get-tuple-element.12.refs_1_, f32[2,640,128]{2,1,0:T(8,128)} %bitcast.4, f32[80,128]{1,0:T(8,128)} %get-tuple-element.14.refs_3_), custom_call_target="tpu_custom_call" | custom-call | tf_op jit(solution)/shard_map/first_update/pallas_call | solution.py:554
  78.8 21.3 %gather.1.refs_0_ = f32[5,8,80,128]{3,2,1,0:T(8,128)} custom-call(f32[80,128]{1,0:T(8,128)} %get-tuple-element.15.prior), custom_call_target="tpu_custom_call" | custom-call | tf_op jit(solution)/shard_map/gather/pallas_call | solution.py:562
  100.1 19.5 %second_update.1 = f32[2,640,128]{2,1,0:T(8,128)} custom-call(f32[5,8,80,128]{3,2,1,0:T(8,128)} %gather.1.refs_0_, f32[5,2,8,1024]{3,2,1,0:T(8,128)} %get-tuple-element.12.refs_1_, f32[2,640,128]{2,1,0:T(8,128)} %get-tuple-element.16.refs_2_), custom_call_target="tpu_custom_call" | custom-call | tf_op jit(solution)/shard_map/second_update/pallas_call | solution.py:571
  119.6 13.8 %spread.1 = f32[10,2,4,2048]{3,2,1,0:T(4,128)} custom-call(f32[2,80,8,128]{3,2,1,0:T(8,128)} %bitcast.3), custom_call_target="tpu_custom_call" | custom-call | tf_op jit(solution)/shard_map/spread/pallas_call | solution.py:579
  133.5 2.0 %copy.8 = f32[10,2,4,2048]{3,2,1,0:T(4,128)} copy(f32[10,2,4,2048]{3,2,1,0:T(4,128)} %spread.1) | data formatting | bytes 1310720

commit v3 on v2

v3 whole, which is shorter than its diff:
```python
import functools

import jax
import jax.numpy as jnp
from jax import lax
from jax.experimental import pallas as pl
from jax.experimental.pallas import tpu as pltpu
from jax.sharding import PartitionSpec as P

BATCHES = 2
REACH = 2
WINDOW = 2 * REACH + 1
SPREAD_RATE = 0.05
EPSILON = 1e-06
MESH = pl.DeviceIdType.MESH
VMEM = pltpu.VMEM
LANES = 128
BLOCK = 256
FORWARD_RIGHT = (2, 1, 3)
ORDER = (2, 1, 3, 0, 4)
F32 = jnp.float32
BF16 = jnp.bfloat16


def rdma(src, dst, send_sem, recv_sem, device):
    return pltpu.make_async_remote_copy(
        src_ref=src,
        dst_ref=dst,
        send_sem=send_sem,
        recv_sem=recv_sem,
        device_id=device,
        device_id_type=MESH,
    )


def greet(devices):
    barrier = pltpu.get_barrier_semaphore()
    for device in devices:
        pl.semaphore_signal(barrier, inc=1, device_id=device, device_id_type=MESH)
    pl.semaphore_wait(barrier, len(devices))


def split2(value):
    high = value.astype(BF16).astype(F32)
    return high, value - high


class Exchange:
    def __init__(self, gathered, send, recv, t, e, nt, ne):
        self.gathered, self.send, self.recv = gathered, send, recv
        self.t, self.e, self.nt = t, e, nt
        self.right, self.left = lax.rem(e + 2, ne), lax.rem(e + ne - 2, ne)
        self.partner = e + 1 - 2 * lax.rem(e, 2)
        self.slots = [
            e,
            self.left,
            self.right,
            lax.rem(e + 4, ne),
            self.partner,
            lax.rem(self.partner + ne - 2, ne),
            lax.rem(self.partner + 2, ne),
            lax.rem(self.partner + 4, ne),
        ]
        self.started = []

    def go(self, k, rel, target_k, target_rel, device):
        copy = rdma(
            self.gathered.at[k, self.slots[rel]],
            self.gathered.at[target_k, self.slots[rel]],
            self.send.at[len(self.started)],
            self.recv.at[target_k, target_rel],
            device,
        )
        copy.start()
        self.started.append(copy)

    def arrive(self, k, rel):
        rdma(
            self.gathered.at[k, self.slots[rel]],
            self.gathered.at[k, self.slots[rel]],
            self.send.at[0],
            self.recv.at[k, rel],
            (self.t, self.partner),
        ).wait_recv()

    def along(self, k):
        self.go(k, 0, k, 1, (self.t, self.right))
        self.go(k, 0, k, 2, (self.t, self.left))
        self.go(k, 0, k, 4, (self.t, self.partner))

    def start(self):
        for offset in (1, -1, 2, -2):
            tile = lax.rem(self.t + self.nt + offset, self.nt)
            self.go(REACH, 0, REACH - offset, 0, (tile, self.e))
        self.along(REACH)

    def tiles(self, ks):
        for k in ks:
            self.arrive(k, 0)
            self.along(k)

    def sides(self, k):
        self.arrive(k, 1)
        if k in FORWARD_RIGHT:
            self.go(k, 1, k, 3, (self.t, self.right))
        self.go(k, 1, k, 5, (self.t, self.partner))
        self.arrive(k, 2)
        if k not in FORWARD_RIGHT:
            self.go(k, 2, k, 3, (self.t, self.left))
        self.go(k, 2, k, 6, (self.t, self.partner))

    def far(self, k):
        self.arrive(k, 3)
        self.go(k, 3, k, 7, (self.t, self.partner))

    def finish(self, k):
        for rel in (4, 5, 6, 7):
            self.arrive(k, rel)


EXCHANGE_SENDS = 4 + 3 * WINDOW + 3 * WINDOW + WINDOW


def tile_peers(t, e, nt):
    return [(lax.rem(t + nt + offset, nt), e) for offset in (1, -1, 2, -2)]


def ens_peers(t, e, ne):
    return [(t, lax.rem(e + d, ne)) for d in range(1, ne)]


def cycle_kernel(
    nt, ne,
    x, u, loc, cnt, val, err, out,
    first, later, cols, meta, grid,
    hs, hr, tmp, ub, bg, parts, sb, rb, second,
    weights, shifts, states, total, closes, gains, ahead,
    halo_s, halo_r, meta_s, meta_r, bulk_s, bulk_r, small_s, small_r,
    first_s, first_r, later_s, later_r, out_s, out_r, own_sem,
):
    t, e = lax.axis_index("tile"), lax.axis_index("ens")
    per, levels, rows, width = x.shape
    lr = levels * rows
    col_count = width // ne
    slots = loc.shape[2]

    def fill(m, carry):
        for l in range(levels):
            hs[0, m, l : l + 1, :] = x[m, l, 0:1, :]
            hs[1, m, l : l + 1, :] = x[m, l, rows - 1 : rows, :]
        return carry

    lax.fori_loop(0, per, fill, 0)
    slot_index = lax.broadcasted_iota(jnp.int32, (1, slots), 1)
    for b in range(BATCHES):
        for i in range(3):
            meta[REACH, b, i : i + 1, :] = loc[i, b : b + 1, :].astype(F32)
        meta[REACH, b, 3:4, :] = val[b : b + 1, :]
        meta[REACH, b, 4:5, :] = err[b : b + 1, :]
        meta[REACH, b, 5:6, :] = (slot_index < cnt[0:1, b : b + 1]).astype(F32)
        meta[REACH, b, 6:8, :] = jnp.zeros((2, slots), F32)
    greet(tile_peers(t, e, nt) + ens_peers(t, e, ne))
    up_tile, down_tile = lax.rem(t + nt - 1, nt), lax.rem(t + 1, nt)
    halos = [
        rdma(hs.at[1], hr.at[0], halo_s.at[0], halo_r.at[0], (down_tile, e)),
        rdma(hs.at[0], hr.at[1], halo_s.at[1], halo_r.at[1], (up_tile, e)),
    ]
    for copy in halos:
        copy.start()
    metas = []
    for i, offset in enumerate((1, -1, 2, -2)):
        copy = rdma(
            meta.at[REACH],
            meta.at[REACH - offset],
            meta_s.at[i],
            meta_r.at[i],
            (lax.rem(t + nt + offset, nt), e),
        )
        copy.start()
        metas.append(copy)
    for a in range(2):
        for l in range(levels):
            ub[a, l * rows : (l + 1) * rows, :] = u[a, l]
    for copy in halos:
        copy.wait_recv()
    has_up = jnp.where(t > 0, 1.0, 0.0).astype(F32)
    has_down = jnp.where(t < nt - 1, 1.0, 0.0).astype(F32)

    def step(m, carry):
        for l in range(levels):
            tmp[l * rows : (l + 1) * rows, :] = x[m, l]
        c = tmp[...]
        above = hr[0, m] * has_up
        below = hr[1, m] * has_down
        row = lax.broadcasted_iota(jnp.int32, (lr, width), 0)
        col = lax.broadcasted_iota(jnp.int32, (lr, width), 1)
        up = pltpu.roll(c, 1, 0)
        down = pltpu.roll(c, lr - 1, 0)
        for l in range(levels):
            up = jnp.where(row == l * rows, above[l : l + 1], up)
            down = jnp.where(row == l * rows + rows - 1, below[l : l + 1], down)
        west = jnp.where(col == 0, 0.0, pltpu.roll(c, 1, 1))
        east = jnp.where(col == width - 1, 0.0, pltpu.roll(c, width - 1, 1))
        wr, wc = ub[0], ub[1]
        tendency = (
            jnp.maximum(wr, 0.0) * (c - up)
            + jnp.minimum(wr, 0.0) * (down - c)
            + jnp.maximum(wc, 0.0) * (c - west)
            + jnp.minimum(wc, 0.0) * (east - c)
        )
        value = c - tendency + SPREAD_RATE * (up + down + west + east - 4.0 * c)
        for i in range(width // LANES):
            bg[i, pl.ds(m * lr, lr), :] = value[:, i * LANES : (i + 1) * LANES]
        return carry

    lax.fori_loop(0, per, step, 0)

    pieces = col_count // LANES

    def block_of(device):
        return pl.ds(device * pieces, pieces)

    def members_of(device):
        return pl.ds(pl.multiple_of(device * per * lr, per * lr), per * lr)

    bulks = []

    def send_bulk(d):
        peer = lax.rem(e + d, ne)
        copy = rdma(
            bg.at[block_of(peer)],
            cols.at[:, members_of(e)],
            bulk_s.at[d],
            bulk_r.at[d],
            (t, peer),
        )
        copy.start()
        bulks.append(copy)

    own = pltpu.make_async_copy(bg.at[block_of(e)], cols.at[:, members_of(e)], own_sem)
    own.start()
    for d in (1, 2, ne - 1, ne - 2):
        send_bulk(d)

    def split(kk, carry):
        f = jnp.concatenate([bg[2 * kk], bg[2 * kk + 1]], axis=1)
        high, rest = split2(f)
        middle, low = split2(rest)
        parts[kk] = jnp.concatenate([high, middle, low], axis=0).astype(BF16)
        return carry

    lax.fori_loop(0, width // BLOCK, split, 0)
    held = per * lr
    for b in range(BATCHES):

        def pick(j, carry):
            here = pl.ds(pl.multiple_of(j * BLOCK, BLOCK), BLOCK)
            place = loc[2, b : b + 1, here] * rows + (loc[0, b : b + 1, here] - t * rows)
            column = loc[1, b : b + 1, here]
            down = lax.broadcasted_iota(jnp.int32, (BLOCK, BLOCK), 0)
            total = jnp.zeros((3 * held, BLOCK), F32)
            for kk in range(width // BLOCK):
                hot = jnp.where(down == column - kk * BLOCK, 1.0, 0.0).astype(BF16)
                total += jnp.dot(parts[kk], hot, preferred_element_type=F32)
            value = total[0:held] + total[held : 2 * held] + total[2 * held :]
            mine = lax.broadcasted_iota(jnp.int32, (lr, BLOCK), 0) == place
            value = jnp.where(mine[None], value.reshape(per, lr, BLOCK), 0.0)
            value = jnp.sum(value, axis=1)
            for half in range(BLOCK // LANES):
                sb[j * (BLOCK // LANES) + half, b, 0:per, :] = value[
                    :, half * LANES : (half + 1) * LANES
                ]
            return carry

        lax.fori_loop(0, slots // BLOCK, pick, 0)

    smalls = []
    for d in (4, 3, 5, 2, 6, 1, 7):
        peer = lax.rem(e + d, ne)
        copy = rdma(sb.at[peer], rb.at[e], small_s.at[d], small_r.at[d], (t, peer))
        copy.start()
        smalls.append(copy)
    for d in (4, 3, 5):
        send_bulk(d)
    rb[e] = sb[e]
    for d in range(1, ne):
        source = lax.rem(e + ne - d, ne)
        rdma(
            sb.at[source], rb.at[source], small_s.at[d], small_r.at[d], (t, source)
        ).wait_recv()
    for s in range(ne):
        first[REACH, e, s * per : (s + 1) * per, :] = rb[s, 0, 0:per, :]
        second[s * per : (s + 1) * per, :] = rb[s, 1, 0:per, :]
    members = per * ne
    halves = pieces
    width = col_count
    span = rows * width
    slot_blocks = slots // BLOCK
    exchanges = [
        Exchange(first, first_s, first_r, t, e, nt, ne),
        Exchange(later, later_s, later_r, t, e, nt, ne),
    ]
    inverse_col = 1.0 / float(x.shape[3] // 2)
    inverse_row = 1.0 / float(REACH * rows)

    def prepare(k, batch):
        gathered = exchanges[batch].gathered

        def piece(s, inner):
            here = pl.ds(pl.multiple_of(s * BLOCK, BLOCK), BLOCK)
            p = jnp.concatenate([gathered[k, 2 * s], gathered[k, 2 * s + 1]], axis=1)
            lev = meta[k, batch, 2:3, here]
            value = meta[k, batch, 3:4, here]
            error = meta[k, batch, 4:5, here]
            live = meta[k, batch, 5:6, here]
            average = jnp.sum(p, axis=0, keepdims=True) / members
            deviation = p - average
            variance = (
                jnp.sum(deviation * deviation, axis=0, keepdims=True) / (members - 1) + EPSILON
            )
            combined = variance + error
            shrink = jnp.sqrt(error / combined)
            mean_post = (error * average + variance * value) / combined
            shift = live * ((shrink - 1.0) * deviation + (mean_post - average))
            weight = deviation * (live / ((members - 1) * variance))
            high, low = split2(weight)
            for l in range(levels):
                factor = jnp.where(lev == float(l), 1.0, 0.5)
                scaled = (high * factor).astype(BF16)
                weights[k, l, 0:members, here] = scaled
                weights[k, l, members : 2 * members, here] = scaled
                weights[k, l, 2 * members : 3 * members, here] = (low * factor).astype(BF16)
            both = jnp.concatenate(split2(shift), axis=0)
            shifts[k, here, :] = both.T.astype(BF16)
            return inner

        lax.fori_loop(0, slot_blocks, piece, 0)

    def cell_major(value):
        high, low = split2(value)
        return jnp.concatenate([high, low, high], axis=0).T.astype(BF16)

    def member_major(value):
        turned = value.T
        return turned[0:members] + turned[members : 2 * members]

    def load_states():
        for i in range(lr):
            here = pl.ds(i, members, stride=lr)
            value = jnp.concatenate([cols[h, here, :] for h in range(halves)], axis=1)
            states[i // rows, i % rows * width : (i % rows + 1) * width, :] = cell_major(value)
        total[...] = jnp.zeros_like(total)

    def store_states():
        for i in range(lr):
            here = pl.ds(i, members, stride=lr)
            change = member_major(total[i * width : (i + 1) * width, :])
            for h in range(halves):
                cols[h, here, :] = cols[h, here, :] + change[:, h * LANES : (h + 1) * LANES]

    def split_gain(gain):
        high = gain.astype(BF16)
        low = (gain - high.astype(F32)).astype(BF16)
        return jnp.concatenate([high, low], axis=1)

    def doubled(k, here):
        right = shifts[k, here, :]
        return jnp.concatenate([right, right], axis=0)

    def look():
        mine = pl.ds(pl.multiple_of(e * LANES, LANES), LANES)
        places = meta[REACH, 1, :, mine].T
        cell_row, cell_col, cell_lev = places[:, 0:1], places[:, 1:2], places[:, 2:3]
        x2 = cell_major(second[...])
        ahead[...] = jnp.zeros_like(ahead)
        for k in range(WINDOW):

            def block(j, inner):
                here = pl.ds(pl.multiple_of(j * BLOCK, BLOCK), BLOCK)
                row_gap = (cell_row - meta[k, 0, 0:1, here]) * inverse_row
                col_gap = (cell_col - meta[k, 0, 1:2, here]) * inverse_col
                close = jnp.maximum(1.0 - row_gap * row_gap - col_gap * col_gap, 0.0)
                low = jnp.dot(x2, weights[k, 0, :, here], preferred_element_type=F32)
                high = jnp.dot(x2, weights[k, 1, :, here], preferred_element_type=F32)
                gain = jnp.where(cell_lev == 0.0, low, high) * (close * close)
                ahead[...] += jnp.dot(
                    split_gain(gain), doubled(k, here), preferred_element_type=F32
                )
                return inner

            lax.fori_loop(0, slot_blocks, block, 0)
        later[REACH, e] = second[...] + member_major(ahead[...])

    def update(k, batch):
        first_cell = 1 if k == 2 * REACH else 0
        last_cell = rows - 1 if k == 0 else rows
        from_cell, to_cell = first_cell * width, last_cell * width
        cells = to_cell - from_cell

        def block(j, inner):
            here = pl.ds(pl.multiple_of(j * BLOCK, BLOCK), BLOCK)
            cell_col = (
                lax.broadcasted_iota(jnp.int32, (width, BLOCK), 0) + e * width
            ).astype(F32) * inverse_col
            col_gap = cell_col - meta[k, batch, 1:2, here] * inverse_col
            col_part = col_gap * col_gap
            obs_row = meta[k, batch, 0:1, here]
            for r in range(first_cell, last_cell):
                row_gap = ((t * rows + r).astype(F32) - obs_row) * inverse_row
                close = jnp.maximum((1.0 - row_gap * row_gap) - col_part, 0.0)
                closes[r * width : (r + 1) * width, :] = close * close
            for l in range(levels):
                covariance = jnp.dot(
                    states[l, from_cell:to_cell, :],
                    weights[k, l, :, here],
                    preferred_element_type=F32,
                )
                gains[l * cells : (l + 1) * cells, :] = split_gain(
                    covariance * closes[from_cell:to_cell, :]
                )
            change = jnp.dot(
                gains[0 : levels * cells, :], doubled(k, here), preferred_element_type=F32
            )
            for l in range(levels):
                total[l * span + from_cell : l * span + to_cell, :] += change[
                    l * cells : (l + 1) * cells
                ]
            return inner

        lax.fori_loop(0, slot_blocks, block, 0)

    now, then = exchanges
    now.start()
    now.tiles((1, 3, 0, 4))
    own.wait()
    for d in range(1, ne):
        source = lax.rem(e + ne - d, ne)
        rdma(
            bg.at[block_of(source)],
            cols.at[:, members_of(source)],
            bulk_s.at[d],
            bulk_r.at[d],
            (t, source),
        ).wait_recv()
    for i, offset in enumerate((1, -1, 2, -2)):
        rdma(
            meta.at[REACH],
            meta.at[REACH - offset],
            meta_s.at[i],
            meta_r.at[i],
            (up_tile, e),
        ).wait_recv()
    load_states()
    now.sides(2)
    now.sides(1)
    now.sides(3)
    now.far(2)
    now.finish(2)
    prepare(2, 0)
    update(2, 0)
    now.sides(0)
    now.sides(4)
    now.far(1)
    now.far(3)
    now.finish(1)
    prepare(1, 0)
    now.far(0)
    now.far(4)
    update(1, 0)
    for k in (3, 0, 4):
        now.finish(k)
        prepare(k, 0)
    look()
    then.start()
    update(3, 0)
    then.tiles((1, 3, 0, 4))
    update(0, 0)
    then.sides(2)
    then.sides(1)
    then.sides(3)
    update(4, 0)
    store_states()
    load_states()
    then.far(2)
    then.sides(0)
    then.sides(4)
    then.finish(2)
    prepare(2, 1)
    then.far(1)
    then.far(3)
    update(2, 1)
    then.far(0)
    then.far(4)
    for k in (1, 3, 0, 4):
        then.finish(k)
        prepare(k, 1)
        update(k, 1)
    store_states()
    copies = []
    for d in (4, 3, 5, 2, 6, 1, 7):
        peer = lax.rem(e + d, ne)
        copy = rdma(
            cols.at[:, members_of(peer)],
            grid.at[block_of(e)],
            out_s.at[d],
            out_r.at[d],
            (t, peer),
        )
        copy.start()
        copies.append(copy)
    home = pltpu.make_async_copy(cols.at[:, members_of(e)], grid.at[block_of(e)], out_s.at[0])
    home.start()
    home.wait()
    for d in range(1, ne):
        source = lax.rem(e + ne - d, ne)
        rdma(
            cols.at[:, members_of(source)],
            grid.at[block_of(source)],
            out_s.at[d],
            out_r.at[d],
            (t, source),
        ).wait_recv()

    def put(m, carry):
        for l in range(levels):
            for i in range(x.shape[3] // LANES):
                out[m, l, :, i * LANES : (i + 1) * LANES] = grid[
                    i, pl.ds(m * lr + l * rows, rows), :
                ]
        return carry

    lax.fori_loop(0, per, put, 0)
    for copy in halos + metas + bulks + smalls + copies + now.started + then.started:
        copy.wait_send()


def on_device(nt, ne, x, u, loc, cnt, val, err):
    per, levels, rows, width = x.shape
    lr = levels * rows
    members = per * ne
    slots = val.shape[1]
    col_count = width // ne
    vmem = pl.BlockSpec(memory_space=VMEM)
    dma = pltpu.SemaphoreType.DMA
    window = VMEM((WINDOW, ne, members, LANES), F32)
    whole = VMEM((width // LANES, per * lr, LANES), F32)
    return pl.pallas_call(
        functools.partial(cycle_kernel, nt, ne),
        out_shape=jax.ShapeDtypeStruct(x.shape, F32),
        in_specs=[vmem] * 6,
        out_specs=vmem,
        scratch_shapes=[
            window,
            window,
            VMEM((col_count // LANES, members * lr, LANES), F32),
            VMEM((WINDOW, BATCHES, 8, slots), F32),
            whole,
            VMEM((2, per, levels, width), F32),
            VMEM((2, per, levels, width), F32),
            VMEM((lr, width), F32),
            VMEM((2, lr, width), F32),
            whole,
            VMEM((width // BLOCK, 3 * per * lr, BLOCK), BF16),
            VMEM((ne, BATCHES, 16, LANES), F32),
            VMEM((ne, BATCHES, 16, LANES), F32),
            VMEM((members, LANES), F32),
            VMEM((WINDOW, levels, 3 * members, slots), BF16),
            VMEM((WINDOW, slots, 2 * members), BF16),
            VMEM((levels, rows * col_count, 3 * members), BF16),
            VMEM((lr * col_count, 2 * members), F32),
            VMEM((rows * col_count, BLOCK), F32),
            VMEM((lr * col_count, 2 * BLOCK), BF16),
            VMEM((LANES, 2 * members), F32),
            dma((2,)),
            dma((2,)),
            dma((4,)),
            dma((4,)),
            dma((ne,)),
            dma((ne,)),
            dma((ne,)),
            dma((ne,)),
            dma((EXCHANGE_SENDS,)),
            dma((WINDOW, ne)),
            dma((EXCHANGE_SENDS,)),
            dma((WINDOW, ne)),
            dma((ne,)),
            dma((ne,)),
            dma,
        ],
        compiler_params=pltpu.CompilerParams(collective_id=0, has_side_effects=True),
        name="cycle",
    )(x, u, loc, cnt.T, val, err)


def solution(mesh):
    in_specs = (
        P("ens", None, "tile", None),
        P(None, None, "tile", None),
        P(None, None, "tile"),
        P(None, "tile"),
        P(None, "tile"),
        P(None, "tile"),
    )
    out_specs = P("ens", None, "tile", None)
    body = functools.partial(on_device, mesh.shape["tile"], mesh.shape["ens"])
    return jax.shard_map(body, mesh=mesh, in_specs=in_specs, out_specs=out_specs, check_vma=False)
```

time: 136 us -> 116 us (0.85)
  Pallas kernels: 133 us -> 114 us
    pallas_call x5 -> x1, Pallas kernels: 133 us -> 114 us  [on_device(): pl.pallas_call(functools.partial(cycle_kernel, nt, ne), out_shape=jax.Sha...]
where the time goes in v3:
time: 116 us
  Pallas kernels  114 us (98%)
  local copies, waits for them, and re-layouts  1.99 us (2%)
    pallas_call x1, Pallas kernels, on_device(): pl.pallas_call(functools.partial(cycle_kernel, nt, ne), out_shape=jax.Sha...  114 us

profile of v3, /device:TPU:1, one launch (start us, length us, event | category | flops | bytes accessed | tf_op | source)
XLA Modules:
  0.0 115.9 jit_solution(3352139000770663331)
XLA Ops:
  0.0 113.9 %cycle.1 = f32[10,2,4,2048]{3,2,1,0:T(4,128)} custom-call(f32[10,2,4,2048]{3,2,1,0:T(4,128)} %x.1, f32[2,2,4,2048]{3,2,1,0:T(4,128)} %u.1, s32[3,2,1024]{2,1,0:T(2,128)} %loc.1, s32[1,2]{1,0:T(1,128)} %bitcast.1, f32[2,1024]{1,0:T(2,128)} %val.1, f32[2,1024]{1,0:T(2,128)} %err.1), custom_call_target="tpu_custom_call" | custom-call | tf_op jit(solution)/shard_map/cycle/pallas_call | solution.py:547
  113.9 2.0 %copy.8 = f32[10,2,4,2048]{3,2,1,0:T(4,128)} copy(f32[10,2,4,2048]{3,2,1,0:T(4,128)} %cycle.1) | data formatting | bytes 1310720

commit v4 on v3

--- a/solution.py
+++ b/solution.py
@@ -132,8 +132,8 @@
 def cycle_kernel(
     nt, ne,
     x, u, loc, cnt, val, err, out,
-    first, later, cols, meta, grid,
-    hs, hr, tmp, ub, bg, parts, sb, rb, second,
+    first, later, cols, meta, leaving, grid,
+    hs, hr, tmp, ub, bg, parts, sb, rb, second, x2,
     weights, shifts, states, total, closes, gains, ahead,
     halo_s, halo_r, meta_s, meta_r, bulk_s, bulk_r, small_s, small_r,
     first_s, first_r, later_s, later_r, out_s, out_r, own_sem,
@@ -251,46 +251,27 @@
 
     lax.fori_loop(0, width // BLOCK, split, 0)
     held = per * lr
-    for b in range(BATCHES):
-
-        def pick(j, carry):
-            here = pl.ds(pl.multiple_of(j * BLOCK, BLOCK), BLOCK)
-            place = loc[2, b : b + 1, here] * rows + (loc[0, b : b + 1, here] - t * rows)
-            column = loc[1, b : b + 1, here]
-            down = lax.broadcasted_iota(jnp.int32, (BLOCK, BLOCK), 0)
-            total = jnp.zeros((3 * held, BLOCK), F32)
-            for kk in range(width // BLOCK):
-                hot = jnp.where(down == column - kk * BLOCK, 1.0, 0.0).astype(BF16)
-                total += jnp.dot(parts[kk], hot, preferred_element_type=F32)
-            value = total[0:held] + total[held : 2 * held] + total[2 * held :]
-            mine = lax.broadcasted_iota(jnp.int32, (lr, BLOCK), 0) == place
-            value = jnp.where(mine[None], value.reshape(per, lr, BLOCK), 0.0)
-            value = jnp.sum(value, axis=1)
-            for half in range(BLOCK // LANES):
-                sb[j * (BLOCK // LANES) + half, b, 0:per, :] = value[
-                    :, half * LANES : (half + 1) * LANES
-                ]
-            return carry
-
-        lax.fori_loop(0, slots // BLOCK, pick, 0)
-
-    smalls = []
-    for d in (4, 3, 5, 2, 6, 1, 7):
-        peer = lax.rem(e + d, ne)
-        copy = rdma(sb.at[peer], rb.at[e], small_s.at[d], small_r.at[d], (t, peer))
-        copy.start()
-        smalls.append(copy)
-    for d in (4, 3, 5):
-        send_bulk(d)
-    rb[e] = sb[e]
-    for d in range(1, ne):
-        source = lax.rem(e + ne - d, ne)
-        rdma(
-            sb.at[source], rb.at[source], small_s.at[d], small_r.at[d], (t, source)
-        ).wait_recv()
-    for s in range(ne):
-        first[REACH, e, s * per : (s + 1) * per, :] = rb[s, 0, 0:per, :]
-        second[s * per : (s + 1) * per, :] = rb[s, 1, 0:per, :]
+    def pick(b, j):
+        here = slice(j * BLOCK, (j + 1) * BLOCK)
+        place = loc[2, b : b + 1, here] * rows + (loc[0, b : b + 1, here] - t * rows)
+        column = loc[1, b : b + 1, here]
+        down = lax.broadcasted_iota(jnp.int32, (BLOCK, BLOCK), 0)
+        picked = jnp.zeros((3 * held, BLOCK), F32)
+        for kk in range(x.shape[3] // BLOCK):
+            hot = jnp.where(down == column - kk * BLOCK, 1.0, 0.0).astype(BF16)
+            picked += jnp.dot(parts[kk], hot, preferred_element_type=F32)
+        value = picked[0:held] + picked[held : 2 * held] + picked[2 * held :]
+        mine = lax.broadcasted_iota(jnp.int32, (lr, BLOCK), 0) == place
+        value = jnp.where(mine[None], value.reshape(per, lr, BLOCK), 0.0)
+        value = jnp.sum(value, axis=1)
+        for half in range(BLOCK // LANES):
+            i = j * (BLOCK // LANES) + half
+            part = value[:, half * LANES : (half + 1) * LANES]
+            if b == 0:
+                first[REACH, e, i * per : (i + 1) * per, :] = part
+            else:
+                sb[i, 0:per, :] = part
+
     members = per * ne
     halves = pieces
     width = col_count
@@ -303,12 +284,23 @@
     inverse_col = 1.0 / float(x.shape[3] // 2)
     inverse_row = 1.0 / float(REACH * rows)
 
+    def prior_of(k, batch, s):
+        if batch:
+            return jnp.concatenate([later[k, 2 * s], later[k, 2 * s + 1]], axis=1)
+        return jnp.concatenate(
+            [
+                jnp.concatenate(
+                    [first[k, d, i * per : (i + 1) * per, :] for d in range(ne)], axis=0
+                )
+                for i in (2 * s, 2 * s + 1)
+            ],
+            axis=1,
+        )
+
     def prepare(k, batch):
-        gathered = exchanges[batch].gathered
-
-        def piece(s, inner):
-            here = pl.ds(pl.multiple_of(s * BLOCK, BLOCK), BLOCK)
-            p = jnp.concatenate([gathered[k, 2 * s], gathered[k, 2 * s + 1]], axis=1)
+        for s in range(slot_blocks):
+            here = slice(s * BLOCK, (s + 1) * BLOCK)
+            p = prior_of(k, batch, s)
             lev = meta[k, batch, 2:3, here]
             value = meta[k, batch, 3:4, here]
             error = meta[k, batch, 4:5, here]
@@ -332,9 +324,6 @@
                 weights[k, l, 2 * members : 3 * members, here] = (low * factor).astype(BF16)
             both = jnp.concatenate(split2(shift), axis=0)
             shifts[k, here, :] = both.T.astype(BF16)
-            return inner
-
-        lax.fori_loop(0, slot_blocks, piece, 0)
 
     def cell_major(value):
         high, low = split2(value)
@@ -351,6 +340,9 @@
             states[i // rows, i % rows * width : (i % rows + 1) * width, :] = cell_major(value)
         total[...] = jnp.zeros_like(total)
 
+    def part_of(device):
+        return pl.ds(pl.multiple_of(device * per * rows, per * rows), per * rows)
+
     def store_states():
         for i in range(lr):
             here = pl.ds(i, members, stride=lr)
@@ -367,31 +359,27 @@
         right = shifts[k, here, :]
         return jnp.concatenate([right, right], axis=0)
 
-    def look():
+    def look(k):
         mine = pl.ds(pl.multiple_of(e * LANES, LANES), LANES)
         places = meta[REACH, 1, :, mine].T
         cell_row, cell_col, cell_lev = places[:, 0:1], places[:, 1:2], places[:, 2:3]
-        x2 = cell_major(second[...])
-        ahead[...] = jnp.zeros_like(ahead)
-        for k in range(WINDOW):
-
-            def block(j, inner):
-                here = pl.ds(pl.multiple_of(j * BLOCK, BLOCK), BLOCK)
-                row_gap = (cell_row - meta[k, 0, 0:1, here]) * inverse_row
-                col_gap = (cell_col - meta[k, 0, 1:2, here]) * inverse_col
-                close = jnp.maximum(1.0 - row_gap * row_gap - col_gap * col_gap, 0.0)
-                low = jnp.dot(x2, weights[k, 0, :, here], preferred_element_type=F32)
-                high = jnp.dot(x2, weights[k, 1, :, here], preferred_element_type=F32)
-                gain = jnp.where(cell_lev == 0.0, low, high) * (close * close)
-                ahead[...] += jnp.dot(
-                    split_gain(gain), doubled(k, here), preferred_element_type=F32
-                )
-                return inner
-
-            lax.fori_loop(0, slot_blocks, block, 0)
-        later[REACH, e] = second[...] + member_major(ahead[...])
-
-    def update(k, batch):
+
+        def block(j, inner):
+            here = pl.ds(pl.multiple_of(j * BLOCK, BLOCK), BLOCK)
+            row_gap = (cell_row - meta[k, 0, 0:1, here]) * inverse_row
+            col_gap = (cell_col - meta[k, 0, 1:2, here]) * inverse_col
+            close = jnp.maximum(1.0 - row_gap * row_gap - col_gap * col_gap, 0.0)
+            factor = jnp.where(meta[k, 0, 2:3, here] == 0.0, 0.5, 2.0)
+            factor = jnp.where(cell_lev == 0.0, 1.0, factor)
+            gain = jnp.dot(x2[...], weights[k, 0, :, here], preferred_element_type=F32)
+            gain = gain * (close * close * factor)
+            ahead[...] += jnp.dot(split_gain(gain), doubled(k, here), preferred_element_type=F32)
+            return inner
+
+        lax.fori_loop(0, slot_blocks, block, 0)
+
+    def update(k, batch, chosen=(0, 1), start=0, stop=None):
+        stop = slot_blocks if stop is None else stop
         first_cell = 1 if k == 2 * REACH else 0
         last_cell = rows - 1 if k == 0 else rows
         from_cell, to_cell = first_cell * width, last_cell * width
@@ -409,29 +397,54 @@
                 row_gap = ((t * rows + r).astype(F32) - obs_row) * inverse_row
                 close = jnp.maximum((1.0 - row_gap * row_gap) - col_part, 0.0)
                 closes[r * width : (r + 1) * width, :] = close * close
-            for l in range(levels):
+            for i, l in enumerate(chosen):
                 covariance = jnp.dot(
                     states[l, from_cell:to_cell, :],
                     weights[k, l, :, here],
                     preferred_element_type=F32,
                 )
-                gains[l * cells : (l + 1) * cells, :] = split_gain(
+                gains[i * cells : (i + 1) * cells, :] = split_gain(
                     covariance * closes[from_cell:to_cell, :]
                 )
             change = jnp.dot(
-                gains[0 : levels * cells, :], doubled(k, here), preferred_element_type=F32
+                gains[0 : len(chosen) * cells, :], doubled(k, here), preferred_element_type=F32
             )
-            for l in range(levels):
+            for i, l in enumerate(chosen):
                 total[l * span + from_cell : l * span + to_cell, :] += change[
-                    l * cells : (l + 1) * cells
+                    i * cells : (i + 1) * cells
                 ]
             return inner
 
-        lax.fori_loop(0, slot_blocks, block, 0)
+        lax.fori_loop(start, stop, block, 0)
 
     now, then = exchanges
+    for j in range(slot_blocks):
+        pick(0, j)
     now.start()
-    now.tiles((1, 3, 0, 4))
+    for d in (4, 3, 5):
+        send_bulk(d)
+    for j in range(slot_blocks):
+        pick(1, j)
+    smalls = []
+    for d in (4, 3, 5, 2, 6, 1, 7):
+        peer = lax.rem(e + d, ne)
+        copy = rdma(sb.at[peer], rb.at[e], small_s.at[d], small_r.at[d], (t, peer))
+        copy.start()
+        smalls.append(copy)
+    rb[e] = sb[e]
+    now.tiles((1, 3))
+    now.sides(2)
+    now.tiles((0, 4))
+    for d in range(1, ne):
+        source = lax.rem(e + ne - d, ne)
+        rdma(
+            sb.at[source], rb.at[source], small_s.at[d], small_r.at[d], (t, source)
+        ).wait_recv()
+    for s in range(ne):
+        second[s * per : (s + 1) * per, :] = rb[s, 0:per, :]
+    x2[...] = cell_major(second[...])
+    ahead[...] = jnp.zeros_like(ahead)
+    now.far(2)
     own.wait()
     for d in range(1, ne):
         source = lax.rem(e + ne - d, ne)
@@ -451,82 +464,95 @@
             (up_tile, e),
         ).wait_recv()
     load_states()
-    now.sides(2)
+    now.finish(2)
+    prepare(2, 0)
+    look(2)
+    update(2, 0, stop=slot_blocks // 2)
     now.sides(1)
     now.sides(3)
-    now.far(2)
-    now.finish(2)
-    prepare(2, 0)
-    update(2, 0)
+    update(2, 0, start=slot_blocks // 2)
+    now.far(1)
+    now.far(3)
     now.sides(0)
     now.sides(4)
-    now.far(1)
-    now.far(3)
     now.finish(1)
     prepare(1, 0)
+    look(1)
     now.far(0)
     now.far(4)
-    update(1, 0)
     for k in (3, 0, 4):
         now.finish(k)
         prepare(k, 0)
-    look()
+        look(k)
+    later[REACH, e] = second[...] + member_major(ahead[...])
     then.start()
+    update(1, 0)
+    then.tiles((1, 3, 0, 4))
+    then.sides(2)
     update(3, 0)
-    then.tiles((1, 3, 0, 4))
-    update(0, 0)
-    then.sides(2)
+    then.far(2)
     then.sides(1)
     then.sides(3)
+    update(0, 0)
+    then.sides(0)
+    then.sides(4)
+    then.far(1)
+    then.far(3)
     update(4, 0)
+    then.far(0)
+    then.far(4)
     store_states()
     load_states()
-    then.far(2)
-    then.sides(0)
-    then.sides(4)
-    then.finish(2)
-    prepare(2, 1)
-    then.far(1)
-    then.far(3)
-    update(2, 1)
-    then.far(0)
-    then.far(4)
-    for k in (1, 3, 0, 4):
+    for k in (2, 1, 3):
         then.finish(k)
         prepare(k, 1)
         update(k, 1)
-    store_states()
-    copies = []
-    for d in (4, 3, 5, 2, 6, 1, 7):
-        peer = lax.rem(e + d, ne)
-        copy = rdma(
-            cols.at[:, members_of(peer)],
-            grid.at[block_of(e)],
-            out_s.at[d],
-            out_r.at[d],
-            (t, peer),
+    for k in (0, 4):
+        then.finish(k)
+        prepare(k, 1)
+    copies, homes = [], []
+    for l in range(levels):
+        update(0, 1, chosen=(l,))
+        update(4, 1, chosen=(l,))
+        for r in range(rows):
+            change = member_major(total[(l * rows + r) * width : (l * rows + r + 1) * width, :])
+            for h in range(halves):
+                leaving[l, h, pl.ds(r, members, stride=rows), :] = (
+                    cols[h, pl.ds(l * rows + r, members, stride=lr), :]
+                    + change[:, h * LANES : (h + 1) * LANES]
+                )
+        for d in (4, 3, 5, 2, 6, 1, 7):
+            peer = lax.rem(e + d, ne)
+            copy = rdma(
+                leaving.at[l, :, part_of(peer)],
+                grid.at[l, block_of(e)],
+                out_s.at[l, d],
+                out_r.at[l, d],
+                (t, peer),
+            )
+            copy.start()
+            copies.append(copy)
+        home = pltpu.make_async_copy(
+            leaving.at[l, :, part_of(e)], grid.at[l, block_of(e)], out_s.at[l, 0]
         )
-        copy.start()
-        copies.append(copy)
-    home = pltpu.make_async_copy(cols.at[:, members_of(e)], grid.at[block_of(e)], out_s.at[0])
-    home.start()
-    home.wait()
-    for d in range(1, ne):
-        source = lax.rem(e + ne - d, ne)
-        rdma(
-            cols.at[:, members_of(source)],
-            grid.at[block_of(source)],
-            out_s.at[d],
-            out_r.at[d],
-            (t, source),
-        ).wait_recv()
+        home.start()
+        homes.append(home)
+    for l in range(levels):
+        homes[l].wait()
+        for d in range(1, ne):
+            source = lax.rem(e + ne - d, ne)
+            rdma(
+                leaving.at[l, :, part_of(source)],
+                grid.at[l, block_of(source)],
+                out_s.at[l, d],
+                out_r.at[l, d],
+                (t, source),
+            ).wait_recv()
 
     def put(m, carry):
         for l in range(levels):
             for i in range(x.shape[3] // LANES):
-                out[m, l, :, i * LANES : (i + 1) * LANES] = grid[
-                    i, pl.ds(m * lr + l * rows, rows), :
-                ]
+                out[m, l, :, i * LANES : (i + 1) * LANES] = grid[l, i, pl.ds(m * rows, rows), :]
         return carry
 
     lax.fori_loop(0, per, put, 0)
@@ -554,16 +580,18 @@
             window,
             VMEM((col_count // LANES, members * lr, LANES), F32),
             VMEM((WINDOW, BATCHES, 8, slots), F32),
-            whole,
+            VMEM((levels, col_count // LANES, members * rows, LANES), F32),
+            VMEM((levels, width // LANES, per * rows, LANES), F32),
             VMEM((2, per, levels, width), F32),
             VMEM((2, per, levels, width), F32),
             VMEM((lr, width), F32),
             VMEM((2, lr, width), F32),
             whole,
             VMEM((width // BLOCK, 3 * per * lr, BLOCK), BF16),
-            VMEM((ne, BATCHES, 16, LANES), F32),
-            VMEM((ne, BATCHES, 16, LANES), F32),
+            VMEM((ne, 16, LANES), F32),
+            VMEM((ne, 16, LANES), F32),
             VMEM((members, LANES), F32),
+            VMEM((LANES, 3 * members), BF16),
             VMEM((WINDOW, levels, 3 * members, slots), BF16),
             VMEM((WINDOW, slots, 2 * members), BF16),
             VMEM((levels, rows * col_count, 3 * members), BF16),
@@ -583,8 +611,8 @@
             dma((WINDOW, ne)),
             dma((EXCHANGE_SENDS,)),
             dma((WINDOW, ne)),
-            dma((ne,)),
-            dma((ne,)),
+            dma((levels, ne)),
+            dma((levels, ne)),
             dma,
         ],
         compiler_params=pltpu.CompilerParams(collective_id=0, has_side_effects=True),

time: 116 us -> 107 us (0.922)
  Pallas kernels: 114 us -> 105 us
    pallas_call x1, Pallas kernels: 114 us -> 105 us  [on_device(): pl.pallas_call(functools.partial(cycle_kernel, nt, ne), out_shape=jax.Sha...]
where the time goes in v4:
time: 107 us
  Pallas kernels  105 us (98%)
  local copies, waits for them, and re-layouts  1.99 us (2%)
    pallas_call x1, Pallas kernels, on_device(): pl.pallas_call(functools.partial(cycle_kernel, nt, ne), out_shape=jax.Sha...  105 us

profile of v4, /device:TPU:1, one launch (start us, length us, event | category | flops | bytes accessed | tf_op | source)
XLA Modules:
  0.0 107.1 jit_solution(406386735718968117)
XLA Ops:
  0.0 105.1 %cycle.1 = f32[10,2,4,2048]{3,2,1,0:T(4,128)} custom-call(f32[10,2,4,2048]{3,2,1,0:T(4,128)} %x.1, f32[2,2,4,2048]{3,2,1,0:T(4,128)} %u.1, s32[3,2,1024]{2,1,0:T(2,128)} %loc.1, s32[1,2]{1,0:T(1,128)} %bitcast.1, f32[2,1024]{1,0:T(2,128)} %val.1, f32[2,1024]{1,0:T(2,128)} %err.1), custom_call_target="tpu_custom_call" | custom-call | tf_op jit(solution)/shard_map/cycle/pallas_call | solution.py:573
  105.1 2.0 %copy.8 = f32[10,2,4,2048]{3,2,1,0:T(4,128)} copy(f32[10,2,4,2048]{3,2,1,0:T(4,128)} %cycle.1) | data formatting | bytes 1310720

commit v5 on v4

--- a/solution.py
+++ b/solution.py
@@ -16,6 +16,7 @@
 VMEM = pltpu.VMEM
 LANES = 128
 BLOCK = 256
+WIDE = 512
 FORWARD_RIGHT = (2, 1, 3)
 ORDER = (2, 1, 3, 0, 4)
 F32 = jnp.float32
@@ -37,7 +38,7 @@
     barrier = pltpu.get_barrier_semaphore()
     for device in devices:
         pl.semaphore_signal(barrier, inc=1, device_id=device, device_id_type=MESH)
-    pl.semaphore_wait(barrier, len(devices))
+    return lambda: pl.semaphore_wait(barrier, len(devices))
 
 
 def split2(value):
@@ -131,12 +132,13 @@
 
 def cycle_kernel(
     nt, ne,
-    x, u, loc, cnt, val, err, out,
+    x_in, u_in, loc, cnt, val, err, out,
+    x, u,
     first, later, cols, meta, leaving, grid,
     hs, hr, tmp, ub, bg, parts, sb, rb, second, x2,
     weights, shifts, states, total, closes, gains, ahead,
     halo_s, halo_r, meta_s, meta_r, bulk_s, bulk_r, small_s, small_r,
-    first_s, first_r, later_s, later_r, out_s, out_r, own_sem,
+    first_s, first_r, later_s, later_r, out_s, out_r, own_sem, in_sem,
 ):
     t, e = lax.axis_index("tile"), lax.axis_index("ens")
     per, levels, rows, width = x.shape
@@ -144,13 +146,13 @@
     col_count = width // ne
     slots = loc.shape[2]
 
-    def fill(m, carry):
-        for l in range(levels):
-            hs[0, m, l : l + 1, :] = x[m, l, 0:1, :]
-            hs[1, m, l : l + 1, :] = x[m, l, rows - 1 : rows, :]
-        return carry
-
-    lax.fori_loop(0, per, fill, 0)
+    inputs = [
+        pltpu.make_async_copy(x_in, x, in_sem.at[0]),
+        pltpu.make_async_copy(u_in, u, in_sem.at[1]),
+    ]
+    for copy in inputs:
+        copy.start()
+    all_here = greet(tile_peers(t, e, nt) + ens_peers(t, e, ne))
     slot_index = lax.broadcasted_iota(jnp.int32, (1, slots), 1)
     for b in range(BATCHES):
         for i in range(3):
@@ -159,7 +161,17 @@
         meta[REACH, b, 4:5, :] = err[b : b + 1, :]
         meta[REACH, b, 5:6, :] = (slot_index < cnt[0:1, b : b + 1]).astype(F32)
         meta[REACH, b, 6:8, :] = jnp.zeros((2, slots), F32)
-    greet(tile_peers(t, e, nt) + ens_peers(t, e, ne))
+    for copy in inputs:
+        copy.wait()
+
+    def fill(m, carry):
+        for l in range(levels):
+            hs[0, m, l : l + 1, :] = x[m, l, 0:1, :]
+            hs[1, m, l : l + 1, :] = x[m, l, rows - 1 : rows, :]
+        return carry
+
+    lax.fori_loop(0, per, fill, 0)
+    all_here()
     up_tile, down_tile = lax.rem(t + nt - 1, nt), lax.rem(t + 1, nt)
     halos = [
         rdma(hs.at[1], hr.at[0], halo_s.at[0], halo_r.at[0], (down_tile, e)),
@@ -378,17 +390,18 @@
 
         lax.fori_loop(0, slot_blocks, block, 0)
 
-    def update(k, batch, chosen=(0, 1), start=0, stop=None):
-        stop = slot_blocks if stop is None else stop
-        first_cell = 1 if k == 2 * REACH else 0
-        last_cell = rows - 1 if k == 0 else rows
+    def update(ks, batch, chosen=(0, 1), start=0, stop=None):
+        first_cell = 1 if ks[0] == 2 * REACH else 0
+        last_cell = rows - 1 if ks[0] == 0 else rows
         from_cell, to_cell = first_cell * width, last_cell * width
-        cells = to_cell - from_cell
-
-        def block(j, inner):
-            here = pl.ds(pl.multiple_of(j * BLOCK, BLOCK), BLOCK)
+        steps = slots // WIDE
+        stop = steps * len(ks) if stop is None else stop
+
+        def block(i, inner):
+            k = ks[0] if len(ks) == 1 else ks[0] + (ks[1] - ks[0]) * (i // steps)
+            here = pl.ds(pl.multiple_of(i % steps * WIDE, WIDE), WIDE)
             cell_col = (
-                lax.broadcasted_iota(jnp.int32, (width, BLOCK), 0) + e * width
+                lax.broadcasted_iota(jnp.int32, (width, WIDE), 0) + e * width
             ).astype(F32) * inverse_col
             col_gap = cell_col - meta[k, batch, 1:2, here] * inverse_col
             col_part = col_gap * col_gap
@@ -397,22 +410,16 @@
                 row_gap = ((t * rows + r).astype(F32) - obs_row) * inverse_row
                 close = jnp.maximum((1.0 - row_gap * row_gap) - col_part, 0.0)
                 closes[r * width : (r + 1) * width, :] = close * close
-            for i, l in enumerate(chosen):
+            right = doubled(k, here)
+            for l in chosen:
                 covariance = jnp.dot(
                     states[l, from_cell:to_cell, :],
                     weights[k, l, :, here],
                     preferred_element_type=F32,
                 )
-                gains[i * cells : (i + 1) * cells, :] = split_gain(
-                    covariance * closes[from_cell:to_cell, :]
-                )
-            change = jnp.dot(
-                gains[0 : len(chosen) * cells, :], doubled(k, here), preferred_element_type=F32
-            )
-            for i, l in enumerate(chosen):
-                total[l * span + from_cell : l * span + to_cell, :] += change[
-                    i * cells : (i + 1) * cells
-                ]
+                mine = slice(l * span + from_cell, l * span + to_cell)
+                gains[mine, :] = split_gain(covariance * closes[from_cell:to_cell, :])
+                total[mine, :] += jnp.dot(gains[mine, :], right, preferred_element_type=F32)
             return inner
 
         lax.fori_loop(start, stop, block, 0)
@@ -467,10 +474,10 @@
     now.finish(2)
     prepare(2, 0)
     look(2)
-    update(2, 0, stop=slot_blocks // 2)
+    update((2,), 0, stop=1)
     now.sides(1)
     now.sides(3)
-    update(2, 0, start=slot_blocks // 2)
+    update((2,), 0, start=1)
     now.far(1)
     now.far(3)
     now.sides(0)
@@ -486,34 +493,37 @@
         look(k)
     later[REACH, e] = second[...] + member_major(ahead[...])
     then.start()
-    update(1, 0)
+    update((1,), 0)
     then.tiles((1, 3, 0, 4))
     then.sides(2)
-    update(3, 0)
+    update((3,), 0)
     then.far(2)
     then.sides(1)
     then.sides(3)
-    update(0, 0)
+    update((0,), 0)
     then.sides(0)
     then.sides(4)
     then.far(1)
     then.far(3)
-    update(4, 0)
+    update((4,), 0)
     then.far(0)
     then.far(4)
     store_states()
     load_states()
-    for k in (2, 1, 3):
+    then.finish(2)
+    prepare(2, 1)
+    update((2,), 1)
+    for k in (1, 3):
         then.finish(k)
         prepare(k, 1)
-        update(k, 1)
+    update((1, 3), 1)
     for k in (0, 4):
         then.finish(k)
         prepare(k, 1)
     copies, homes = [], []
     for l in range(levels):
-        update(0, 1, chosen=(l,))
-        update(4, 1, chosen=(l,))
+        update((0,), 1, chosen=(l,))
+        update((4,), 1, chosen=(l,))
         for r in range(rows):
             change = member_major(total[(l * rows + r) * width : (l * rows + r + 1) * width, :])
             for h in range(halves):
@@ -573,9 +583,11 @@
     return pl.pallas_call(
         functools.partial(cycle_kernel, nt, ne),
         out_shape=jax.ShapeDtypeStruct(x.shape, F32),
-        in_specs=[vmem] * 6,
+        in_specs=[pl.BlockSpec(memory_space=pl.ANY)] * 2 + [vmem] * 4,
         out_specs=vmem,
         scratch_shapes=[
+            VMEM(x.shape, F32),
+            VMEM(u.shape, F32),
             window,
             window,
             VMEM((col_count // LANES, members * lr, LANES), F32),
@@ -596,8 +608,8 @@
             VMEM((WINDOW, slots, 2 * members), BF16),
             VMEM((levels, rows * col_count, 3 * members), BF16),
             VMEM((lr * col_count, 2 * members), F32),
-            VMEM((rows * col_count, BLOCK), F32),
-            VMEM((lr * col_count, 2 * BLOCK), BF16),
+            VMEM((rows * col_count, WIDE), F32),
+            VMEM((lr * col_count, 2 * WIDE), BF16),
             VMEM((LANES, 2 * members), F32),
             dma((2,)),
             dma((2,)),
@@ -614,6 +626,7 @@
             dma((levels, ne)),
             dma((levels, ne)),
             dma,
+            dma((2,)),
         ],
         compiler_params=pltpu.CompilerParams(collective_id=0, has_side_effects=True),
         name="cycle",

time: 107 us -> 104 us (0.972)
  Pallas kernels: 105 us -> 102 us
    pallas_call x1, Pallas kernels: 105 us -> 102 us  [on_device(): pl.pallas_call(functools.partial(cycle_kernel, nt, ne), out_shape=jax.Sha...]
where the time goes in v5:
time: 104 us
  Pallas kernels  102 us (98%)
  local copies, waits for them, and re-layouts  1.99 us (2%)
    pallas_call x1, Pallas kernels, on_device(): pl.pallas_call(functools.partial(cycle_kernel, nt, ne), out_shape=jax.Sha...  102 us

profile of v5, /device:TPU:1, one launch (start us, length us, event | category | flops | bytes accessed | tf_op | source)
XLA Modules:
  0.0 103.9 jit_solution(11785658377467262149)
XLA Ops:
  0.0 101.9 %cycle.1 = f32[10,2,4,2048]{3,2,1,0:T(4,128)} custom-call(f32[10,2,4,2048]{3,2,1,0:T(4,128)} %x_in.1, f32[2,2,4,2048]{3,2,1,0:T(4,128)} %u_in.1, s32[3,2,1024]{2,1,0:T(2,128)} %loc.1, s32[1,2]{1,0:T(1,128)} %bitcast.1, f32[2,1024]{1,0:T(2,128)} %val.1, f32[2,1024]{1,0:T(2,128)} %err.1), custom_call_target="tpu_custom_call" | custom-call | tf_op jit(solution)/shard_map/cycle/pallas_call | solution.py:583
  101.9 2.0 %copy.8 = f32[10,2,4,2048]{3,2,1,0:T(4,128)} copy(f32[10,2,4,2048]{3,2,1,0:T(4,128)} %cycle.1) | data formatting | bytes 1310720

commit v6 on v5

--- a/solution.py
+++ b/solution.py
@@ -328,12 +328,11 @@
             shift = live * ((shrink - 1.0) * deviation + (mean_post - average))
             weight = deviation * (live / ((members - 1) * variance))
             high, low = split2(weight)
-            for l in range(levels):
-                factor = jnp.where(lev == float(l), 1.0, 0.5)
-                scaled = (high * factor).astype(BF16)
-                weights[k, l, 0:members, here] = scaled
-                weights[k, l, members : 2 * members, here] = scaled
-                weights[k, l, 2 * members : 3 * members, here] = (low * factor).astype(BF16)
+            factor = jnp.where(lev == 0.0, 1.0, 0.5)
+            scaled = (high * factor).astype(BF16)
+            weights[k, 0:members, here] = scaled
+            weights[k, members : 2 * members, here] = scaled
+            weights[k, 2 * members : 3 * members, here] = (low * factor).astype(BF16)
             both = jnp.concatenate(split2(shift), axis=0)
             shifts[k, here, :] = both.T.astype(BF16)
 
@@ -383,7 +382,7 @@
             close = jnp.maximum(1.0 - row_gap * row_gap - col_gap * col_gap, 0.0)
             factor = jnp.where(meta[k, 0, 2:3, here] == 0.0, 0.5, 2.0)
             factor = jnp.where(cell_lev == 0.0, 1.0, factor)
-            gain = jnp.dot(x2[...], weights[k, 0, :, here], preferred_element_type=F32)
+            gain = jnp.dot(x2[...], weights[k, :, here], preferred_element_type=F32)
             gain = gain * (close * close * factor)
             ahead[...] += jnp.dot(split_gain(gain), doubled(k, here), preferred_element_type=F32)
             return inner
@@ -414,11 +413,14 @@
             for l in chosen:
                 covariance = jnp.dot(
                     states[l, from_cell:to_cell, :],
-                    weights[k, l, :, here],
+                    weights[k, :, here],
                     preferred_element_type=F32,
                 )
                 mine = slice(l * span + from_cell, l * span + to_cell)
-                gains[mine, :] = split_gain(covariance * closes[from_cell:to_cell, :])
+                gain = covariance * closes[from_cell:to_cell, :]
+                if l:
+                    gain = gain * jnp.where(meta[k, batch, 2:3, here] == 0.0, 0.5, 2.0)
+                gains[mine, :] = split_gain(gain)
                 total[mine, :] += jnp.dot(gains[mine, :], right, preferred_element_type=F32)
             return inner
 
@@ -428,8 +430,6 @@
     for j in range(slot_blocks):
         pick(0, j)
     now.start()
-    for d in (4, 3, 5):
-        send_bulk(d)
     for j in range(slot_blocks):
         pick(1, j)
     smalls = []
@@ -439,9 +439,10 @@
         copy.start()
         smalls.append(copy)
     rb[e] = sb[e]
+    now.sides(2)
+    for d in (4, 3, 5):
+        send_bulk(d)
     now.tiles((1, 3))
-    now.sides(2)
-    now.tiles((0, 4))
     for d in range(1, ne):
         source = lax.rem(e + ne - d, ne)
         rdma(
@@ -452,6 +453,18 @@
     x2[...] = cell_major(second[...])
     ahead[...] = jnp.zeros_like(ahead)
     now.far(2)
+    now.tiles((0, 4))
+    for i, offset in enumerate((1, -1, 2, -2)):
+        rdma(
+            meta.at[REACH],
+            meta.at[REACH - offset],
+            meta_s.at[i],
+            meta_r.at[i],
+            (up_tile, e),
+        ).wait_recv()
+    now.finish(2)
+    prepare(2, 0)
+    look(2)
     own.wait()
     for d in range(1, ne):
         source = lax.rem(e + ne - d, ne)
@@ -462,18 +475,7 @@
             bulk_r.at[d],
             (t, source),
         ).wait_recv()
-    for i, offset in enumerate((1, -1, 2, -2)):
-        rdma(
-            meta.at[REACH],
-            meta.at[REACH - offset],
-            meta_s.at[i],
-            meta_r.at[i],
-            (up_tile, e),
-        ).wait_recv()
     load_states()
-    now.finish(2)
-    prepare(2, 0)
-    look(2)
     update((2,), 0, stop=1)
     now.sides(1)
     now.sides(3)
@@ -604,7 +606,7 @@
             VMEM((ne, 16, LANES), F32),
             VMEM((members, LANES), F32),
             VMEM((LANES, 3 * members), BF16),
-            VMEM((WINDOW, levels, 3 * members, slots), BF16),
+            VMEM((WINDOW, 3 * members, slots), BF16),
             VMEM((WINDOW, slots, 2 * members), BF16),
             VMEM((levels, rows * col_count, 3 * members), BF16),
             VMEM((lr * col_count, 2 * members), F32),

time: 104 us -> 103 us (level)
  no operation moved by 1% of the time
where the time goes in v6:
time: 103 us
  Pallas kernels  101 us (98%)
  local copies, waits for them, and re-layouts  1.99 us (2%)
    pallas_call x1, Pallas kernels, on_device(): pl.pallas_call(functools.partial(cycle_kernel, nt, ne), out_shape=jax.Sha...  101 us

profile of v6, /device:TPU:1, one launch (start us, length us, event | category | flops | bytes accessed | tf_op | source)
XLA Modules:
  0.0 103.1 jit_solution(16035549443156938117)
XLA Ops:
  0.0 101.2 %cycle.1 = f32[10,2,4,2048]{3,2,1,0:T(4,128)} custom-call(f32[10,2,4,2048]{3,2,1,0:T(4,128)} %x_in.1, f32[2,2,4,2048]{3,2,1,0:T(4,128)} %u_in.1, s32[3,2,1024]{2,1,0:T(2,128)} %loc.1, s32[1,2]{1,0:T(1,128)} %bitcast.1, f32[2,1024]{1,0:T(2,128)} %val.1, f32[2,1024]{1,0:T(2,128)} %err.1), custom_call_target="tpu_custom_call" | custom-call | tf_op jit(solution)/shard_map/cycle/pallas_call | solution.py:585
  101.2 2.0 %copy.8 = f32[10,2,4,2048]{3,2,1,0:T(4,128)} copy(f32[10,2,4,2048]{3,2,1,0:T(4,128)} %cycle.1) | data formatting | bytes 1310720
